TPU v7x, 32 devices: a whole 2x2x4 slice. The times are simulated.
32 devices in a mesh: grp: 8 (over y, x, core), seq: 4 (over z).
Axes of the slice: x: 2, y: 2, z: 4, core: 2. Of those that a mesh axis runs over, the one named last changes fastest.
Arguments:
- tokens: bfloat16 [16384, 1024], P(('grp', 'seq')), may hold values from -6 to 6
- cotangent: bfloat16 [16384, 1024], P(('grp', 'seq')), may hold values from -6 to 6
- image_of_token: int32 [16384], P('grp'), may hold values from 0 to 3, as said below
- ln1_gain: bfloat16 [1024], P(('grp', 'seq')), may hold values from 0.5 to 1.5
- ln1_bias: bfloat16 [1024], P(('grp', 'seq')), may hold values from -2 to 2
- qkv_weight: bfloat16 [1024, 3072], P(('grp', 'seq')), may hold values from -0.1875 to 0.1875
- q_bias: bfloat16 [1024], P(('grp', 'seq')), may hold values from -2 to 2
- v_bias: bfloat16 [1024], P(('grp', 'seq')), may hold values from -2 to 2
- out_weight: bfloat16 [1024, 1024], P(('grp', 'seq')), may hold values from -0.75 to 0.75
- out_bias: bfloat16 [1024], P(('grp', 'seq')), may hold values from -2 to 2
- ln2_gain: bfloat16 [1024], P(('grp', 'seq')), may hold values from 0.5 to 1.5
- ln2_bias: bfloat16 [1024], P(('grp', 'seq')), may hold values from -2 to 2
- up_weight: bfloat16 [1024, 4096], P(('grp', 'seq')), may hold values from -0.1875 to 0.1875
- up_bias: bfloat16 [4096], P(('grp', 'seq')), may hold values from -3 to 3
- down_weight: bfloat16 [4096, 1024], P(('grp', 'seq')), may hold values from -0.09375 to 0.09375
- down_bias: bfloat16 [1024], P(('grp', 'seq')), may hold values from -2 to 2
Outputs:
- output: bfloat16 [16384, 1024], P(('grp', 'seq'))
- input_grad: bfloat16 [16384, 1024], P(('grp', 'seq'))
- ln1_gain_grad: float32 [1024], P(('grp', 'seq'))
- ln1_bias_grad: float32 [1024], P(('grp', 'seq'))
- qkv_weight_grad: float32 [1024, 3072], P(('grp', 'seq'))
- q_bias_grad: float32 [1024], P(('grp', 'seq'))
- v_bias_grad: float32 [1024], P(('grp', 'seq'))
- out_weight_grad: float32 [1024, 1024], P(('grp', 'seq'))
- out_bias_grad: float32 [1024], P(('grp', 'seq'))
- ln2_gain_grad: float32 [1024], P(('grp', 'seq'))
- ln2_bias_grad: float32 [1024], P(('grp', 'seq'))
- up_weight_grad: float32 [1024, 4096], P(('grp', 'seq'))
- up_bias_grad: float32 [4096], P(('grp', 'seq'))
- down_weight_grad: float32 [4096, 1024], P(('grp', 'seq'))
- down_bias_grad: float32 [1024], P(('grp', 'seq'))
Inputs may be any that keep to these rules, and one draw needn't show every extreme that they name: `image_of_token`: each group of 2048 slots (one index of grp) holds 1 to 3 whole images of 577 tokens, numbered 0, 1, ... from its first slot; the rest of its slots are marked 3 and attend to one another; some group holds 3 images.
All inputs are finite; a program needn't handle non-finite values.
Results may differ from a plain program's by a relative error of at most 0.012.
Values may be sent and summed in bfloat16 or wider, within the bound.
A program may use at most 192 MiB of HBM per device.

v0:
```python
from functools import partial
import math

import jax
import jax.numpy as jnp
from jax import lax
from jax.sharding import PartitionSpec as P

HEADS = 16


EPS = 1e-06
MASKED = -1e30
HEAD_BLOCK = 4


def layer_norm(value, gain, shift):
    center = value - jnp.mean(value, axis=-1, keepdims=True)
    spread = jnp.mean(center * center, axis=-1, keepdims=True)
    return center * lax.rsqrt(spread + EPS) * gain + shift


def scaled_norm(value, gain):
    return layer_norm(value, gain, 0.0)


def rows_dot(left, right):
    return lax.dot_general(
        left, right, (((0,), (0,)), ((), ())), preferred_element_type=jnp.float32
    )


def dot_back(left, right):
    return lax.dot_general(
        left, right, (((1,), (1,)), ((), ())), preferred_element_type=jnp.float32
    )


def split_heads(rows):
    count, width = rows.shape
    return rows.reshape(count, HEADS // HEAD_BLOCK, HEAD_BLOCK, width // HEADS).transpose(
        1, 0, 2, 3
    )


def join_heads(parts):
    blocks, count, inner, size = parts.shape
    return parts.transpose(1, 0, 2, 3).reshape(count, blocks * inner * size)


def block_scores(query, keys, same):
    scale = 1.0 / math.sqrt(query.shape[-1])
    scores = jnp.einsum("qhd,khd->hqk", query, keys, preferred_element_type=jnp.float32) * scale
    return (jnp.where(same[None], scores, MASKED), scale)


def attend_block(query, keys, values, same):
    scores, scale = block_scores(query, keys, same)
    peak = jnp.max(scores, axis=-1, keepdims=True)
    expo = jnp.exp(scores - peak)
    total = jnp.sum(expo, axis=-1, keepdims=True)
    probs = (expo / total).astype(jnp.bfloat16)
    result = jnp.einsum("hqk,khd->qhd", probs, values, preferred_element_type=jnp.float32)
    return (result, peak[..., 0] + jnp.log(total[..., 0]))


def score_grads(query, keys, values, same, spread, grad_out):
    scores, scale = block_scores(query, keys, same)
    weights = jnp.exp(scores - spread[..., None])
    grad_probs = jnp.einsum("qhd,khd->hqk", grad_out, values, preferred_element_type=jnp.float32)
    inner = jnp.sum(weights * grad_probs, axis=-1)
    grad_scores = (weights * (grad_probs - inner[..., None])).astype(jnp.bfloat16)
    return (weights, grad_scores, inner, scale)


def attend_back(query, keys, values, same, spread, grad_out):
    weights, grad_scores, inner, scale = score_grads(query, keys, values, same, spread, grad_out)
    grad_query = (
        jnp.einsum("hqk,khd->qhd", grad_scores, keys, preferred_element_type=jnp.float32) * scale
    )
    grad_keys = (
        jnp.einsum("hqk,qhd->khd", grad_scores, query, preferred_element_type=jnp.float32) * scale
    )
    grad_values = jnp.einsum(
        "hqk,qhd->khd", weights.astype(jnp.bfloat16), grad_out, preferred_element_type=jnp.float32
    )
    return (grad_query, grad_keys, grad_values)


def per_device(
    tokens,
    cotangent,
    image_of_token,
    ln1_gain,
    ln1_bias,
    qkv_weight,
    q_bias,
    v_bias,
    out_weight,
    out_bias,
    ln2_gain,
    ln2_bias,
    up_weight,
    up_bias,
    down_weight,
    down_bias,
):
    f32 = jnp.float32
    bf16 = jnp.bfloat16
    width = tokens.shape[1]
    local = tokens.shape[0]
    gathered = (
        lax.all_gather(ln1_gain, ("grp", "seq"), axis=0, tiled=True),
        lax.all_gather(ln1_bias, ("grp", "seq"), axis=0, tiled=True),
        lax.all_gather(qkv_weight, ("grp", "seq"), axis=0, tiled=True),
        lax.all_gather(q_bias, ("grp", "seq"), axis=0, tiled=True),
        lax.all_gather(v_bias, ("grp", "seq"), axis=0, tiled=True),
        lax.all_gather(out_weight, ("grp", "seq"), axis=0, tiled=True),
        lax.all_gather(out_bias, ("grp", "seq"), axis=0, tiled=True),
        lax.all_gather(ln2_gain, ("grp", "seq"), axis=0, tiled=True),
        lax.all_gather(ln2_bias, ("grp", "seq"), axis=0, tiled=True),
        lax.all_gather(up_weight, ("grp", "seq"), axis=0, tiled=True),
        lax.all_gather(up_bias, ("grp", "seq"), axis=0, tiled=True),
        lax.all_gather(down_weight, ("grp", "seq"), axis=0, tiled=True),
        lax.all_gather(down_bias, ("grp", "seq"), axis=0, tiled=True),
    )
    (
        gain_first,
        shift_first,
        w_joint,
        bias_query,
        bias_value,
        w_out,
        bias_out,
        gain_second,
        shift_second,
        w_up,
        bias_up,
        w_down,
        bias_down,
    ) = gathered
    inputs = tokens.astype(f32)
    normed_first = layer_norm(inputs, gain_first.astype(f32), shift_first.astype(f32)).astype(bf16)
    zeros = jnp.zeros((width,), f32)
    joint_bias = jnp.concatenate([bias_query.astype(f32), zeros, bias_value.astype(f32)])
    joint = (jnp.dot(normed_first, w_joint, preferred_element_type=f32) + joint_bias).astype(bf16)
    queries = joint[:, :width]
    keys = joint[:, width : 2 * width]
    values = joint[:, 2 * width :]
    all_keys, all_values = (
        lax.all_gather(keys, "seq", axis=0, tiled=True),
        lax.all_gather(values, "seq", axis=0, tiled=True),
    )
    start = lax.axis_index("seq") * local
    own_labels = lax.dynamic_slice_in_dim(image_of_token, start, local)
    same = own_labels[:, None] == image_of_token[None, :]
    query_parts = split_heads(queries)
    key_parts = split_heads(all_keys)
    value_parts = split_heads(all_values)

    def forward_block(item):
        return attend_block(item[0], item[1], item[2], same)

    attended_parts, spread = lax.map(forward_block, (query_parts, key_parts, value_parts))
    attended = join_heads(attended_parts).astype(bf16)
    resid = inputs + jnp.dot(attended, w_out, preferred_element_type=f32) + bias_out.astype(f32)
    normed_second = layer_norm(resid, gain_second.astype(f32), shift_second.astype(f32)).astype(
        bf16
    )
    hidden = jnp.dot(normed_second, w_up, preferred_element_type=f32) + bias_up.astype(f32)
    active = jax.nn.gelu(hidden, approximate=False).astype(bf16)
    output = (
        resid + jnp.dot(active, w_down, preferred_element_type=f32) + bias_down.astype(f32)
    ).astype(bf16)
    gain_first, w_joint, w_out, gain_second, w_up, w_down = (
        lax.all_gather(ln1_gain, ("grp", "seq"), axis=0, tiled=True),
        lax.all_gather(qkv_weight, ("grp", "seq"), axis=0, tiled=True),
        lax.all_gather(out_weight, ("grp", "seq"), axis=0, tiled=True),
        lax.all_gather(ln2_gain, ("grp", "seq"), axis=0, tiled=True),
        lax.all_gather(up_weight, ("grp", "seq"), axis=0, tiled=True),
        lax.all_gather(down_weight, ("grp", "seq"), axis=0, tiled=True),
    )
    down_grad = rows_dot(active, cotangent)
    down_bias_grad = jnp.sum(cotangent.astype(f32), axis=0)
    grad_active = dot_back(cotangent, w_down)
    _, gelu_back = jax.vjp(partial(jax.nn.gelu, approximate=False), hidden)
    grad_hidden = gelu_back(grad_active)[0].astype(bf16)
    up_grad = rows_dot(normed_second, grad_hidden)
    up_bias_grad = jnp.sum(grad_hidden.astype(f32), axis=0)
    grad_normed = dot_back(grad_hidden, w_up)
    _, second_back = jax.vjp(scaled_norm, resid, gain_second.astype(f32))
    grad_through, gain_second_grad = second_back(grad_normed)
    shift_second_grad = jnp.sum(grad_normed, axis=0)
    grad_resid = cotangent.astype(f32) + grad_through
    grad_branch = grad_resid.astype(bf16)
    out_grad = rows_dot(attended, grad_branch)
    out_bias_grad = jnp.sum(grad_branch.astype(f32), axis=0)
    grad_attended = dot_back(grad_branch, w_out).astype(bf16)
    back_keys, back_values = (
        lax.all_gather(keys, "seq", axis=0, tiled=True),
        lax.all_gather(values, "seq", axis=0, tiled=True),
    )
    key_parts = split_heads(back_keys)
    value_parts = split_heads(back_values)
    grad_parts = split_heads(grad_attended)

    def backward_block(item):
        return attend_back(item[0], item[1], item[2], same, item[3], item[4])

    grad_q_parts, grad_k_parts, grad_v_parts = lax.map(
        backward_block, (query_parts, key_parts, value_parts, spread, grad_parts)
    )
    grad_keys, grad_values = (
        lax.psum_scatter(
            join_heads(grad_k_parts).astype(jnp.bfloat16), "seq", scatter_dimension=0, tiled=True
        ).astype(jnp.float32),
        lax.psum_scatter(
            join_heads(grad_v_parts).astype(jnp.bfloat16), "seq", scatter_dimension=0, tiled=True
        ).astype(jnp.float32),
    )
    grad_queries = join_heads(grad_q_parts)
    grad_joint = jnp.concatenate([grad_queries, grad_keys, grad_values], axis=1).astype(bf16)
    joint_grad = rows_dot(normed_first, grad_joint)
    column_sums = jnp.sum(grad_joint.astype(f32), axis=0)
    query_bias_grad = column_sums[:width]
    value_bias_grad = column_sums[2 * width :]
    grad_first = dot_back(grad_joint, w_joint)
    _, first_back = jax.vjp(scaled_norm, inputs, gain_first.astype(f32))
    grad_entry, gain_first_grad = first_back(grad_first)
    shift_first_grad = jnp.sum(grad_first, axis=0)
    input_grad = (grad_resid + grad_entry).astype(bf16)
    summed = (
        lax.psum_scatter(gain_first_grad, ("grp", "seq"), scatter_dimension=0, tiled=True),
        lax.psum_scatter(shift_first_grad, ("grp", "seq"), scatter_dimension=0, tiled=True),
        lax.psum_scatter(joint_grad, ("grp", "seq"), scatter_dimension=0, tiled=True),
        lax.psum_scatter(query_bias_grad, ("grp", "seq"), scatter_dimension=0, tiled=True),
        lax.psum_scatter(value_bias_grad, ("grp", "seq"), scatter_dimension=0, tiled=True),
        lax.psum_scatter(out_grad, ("grp", "seq"), scatter_dimension=0, tiled=True),
        lax.psum_scatter(out_bias_grad, ("grp", "seq"), scatter_dimension=0, tiled=True),
        lax.psum_scatter(gain_second_grad, ("grp", "seq"), scatter_dimension=0, tiled=True),
        lax.psum_scatter(shift_second_grad, ("grp", "seq"), scatter_dimension=0, tiled=True),
        lax.psum_scatter(up_grad, ("grp", "seq"), scatter_dimension=0, tiled=True),
        lax.psum_scatter(up_bias_grad, ("grp", "seq"), scatter_dimension=0, tiled=True),
        lax.psum_scatter(down_grad, ("grp", "seq"), scatter_dimension=0, tiled=True),
        lax.psum_scatter(down_bias_grad, ("grp", "seq"), scatter_dimension=0, tiled=True),
    )
    return (output, input_grad) + tuple(summed)


def solution(mesh):
    placed = (
        P(("grp", "seq"), None),
        P(("grp", "seq"), None),
        P("grp"),
        P(("grp", "seq")),
        P(("grp", "seq")),
        P(("grp", "seq"), None),
        P(("grp", "seq")),
        P(("grp", "seq")),
        P(("grp", "seq"), None),
        P(("grp", "seq")),
        P(("grp", "seq")),
        P(("grp", "seq")),
        P(("grp", "seq"), None),
        P(("grp", "seq")),
        P(("grp", "seq"), None),
        P(("grp", "seq")),
    )
    return jax.shard_map(
        per_device,
        mesh=mesh,
        in_specs=placed,
        out_specs=(
            P(("grp", "seq"), None),
            P(("grp", "seq"), None),
            P(("grp", "seq")),
            P(("grp", "seq")),
            P(("grp", "seq"), None),
            P(("grp", "seq")),
            P(("grp", "seq")),
            P(("grp", "seq"), None),
            P(("grp", "seq")),
            P(("grp", "seq")),
            P(("grp", "seq")),
            P(("grp", "seq"), None),
            P(("grp", "seq")),
            P(("grp", "seq"), None),
            P(("grp", "seq")),
        ),
        check_vma=False,
    )
```

profile of v0, /device:TPU:0, one launch (start us, length us, event | category | flops | bytes accessed | tf_op | source)
XLA Modules:
  0.0 1946.0 jit_solution(4560863303652651203)
XLA Ops:
  14.7 42.7 %all-reduce.18 = (bf16[1024]{0:T(1024)(128)(2,1)S(1)}, bf16[1024]{0:T(1024)(128)(2,1)S(1)}, bf16[1024]{0:T(1024)(128)(2,1)S(1)}, bf16[1024]{0:T(1024)(128)(2,1)S...) all-reduce(bf16[1024]{0:T(1024)(128)(2,1)S(1)} %dynamic-update-slic, ...), channel_id=1, replica_groups=mesh['grp'=8,'seq'=4] {'grp','seq'}, use_global_device_ids=true, to_apply=%add.3 | all-reduce | flops 8192 | bytes 32768
  61.4 21.9 %all-gather.8.cloned.1.call-done = bf16[1024,3072]{1,0:T(8,128)(2,1)} async-done(((bf16[32,3072]{1,0:T(8,128)(2,1)}), bf16[1024,3072]{1,0:T(8,128)(2,1)}) %all-gather.8.cloned.1.call-update) | async-done | bytes 6291472 | tf_op jit(solution)/shard_map/all_gather | solution.py:115
  83.3 6.7 add_convert_fusion.1
  96.1 66.8 %all-gather = bf16[32,1,128]{2,1,0:T(2,128)(2,1)S(1)} all-gather(bf16[1,1,128]{2,1,0:T(2,128)(2,1)S(1)} %bitcast.159), channel_id=1, replica_groups=mesh['grp'=8,'seq'=4] {'grp','seq'}, dimensions={0}, use_global_device_ids=true | all-gather | bytes 8448 | tf_op jit(solution)/shard_map/all_gather | solution.py:123
  164.1 7.2 all-gather.10.cloned.1.call-done
  171.3 6.5 copy.39
  177.8 75.0 %all-gather.12.cloned.1.call-done = bf16[2048,1024]{1,0:T(8,128)(2,1)} async-done(((bf16[512,1024]{1,0:T(8,128)(2,1)}), bf16[2048,1024]{1,0:T(8,128)(2,1)}) %all-gather.12.cloned.1.call-update) | async-done | bytes 4194320 | tf_op jit(solution)/shard_map/all_gather | solution.py:151
  252.8 6.5 copy.41
  259.5 65.9 %while.28 = (s32[]{:T(128)}, bf16[4,512,4,64]{1,3,2,0:T(8,128)(2,1)S(1)}, f32[4,4,512]{2,1,0:T(4,128)}, bf16[4,2048,4,64]{1,3,2,0:T(8,128)(2,1)}, bf16[4,512,4,6...) while((s32[]{:T(128)}, ...), condition=%wide.region_5.6_spmd.clone, body=%wide.region_2.5_spmd.clone.sunk | while | flops 1125120000 | bytes 57487464 | solution.py:164
  269.0 6.3 fusion.133
  285.5 6.3 fusion.133
  301.9 6.3 fusion.133
  318.4 6.3 fusion.133
  330.4 59.4 %all-gather.16.cloned.1.call-done = bf16[1024,4096]{1,0:T(8,128)(2,1)} async-done(((bf16[32,4096]{1,0:T(8,128)(2,1)}), bf16[1024,4096]{1,0:T(8,128)(2,1)}) %all-gather.16.cloned.1.call-update) | async-done | bytes 8388624 | tf_op jit(solution)/shard_map/all_gather | solution.py:122
  389.8 10.3 fusion.84
  400.1 68.5 %all-gather.18.cloned.1.call-done = bf16[4096,1024]{1,0:T(8,128)(2,1)} async-done(((bf16[128,1024]{1,0:T(8,128)(2,1)}), bf16[4096,1024]{1,0:T(8,128)(2,1)}) %all-gather.18.cloned.1.call-update) | async-done | bytes 8388624 | tf_op jit(solution)/shard_map/all_gather | solution.py:124
  468.6 28.6 %convert_reduce_fusion = (f32[4096]{0:T(1024)}, bf16[512,4096]{1,0:T(8,128)(2,1)S(1)}, f32[512,4096]{1,0:T(8,128)}) fusion(f32[512,4096]{1,0:T(8,128)} %fusion.84, f32[4096]{0:T(1024)S(1)} %bitcast.157, bf16[512,1024]{1,0:T(8,128)(2,1)S(1)} %copy-done.8, bf16[4096,1024]{1,0:T(8,128)(2,1)} %all-gather.18.cloned.1.call-done), kind=kOutput, calls=%fused_computation.64 | convolution fusion | flops 4452249600 | bytes 30441472 | tf_op jit(solution)/shard_map/dot_general | solution.py:34
  508.7 231.7 %while.29 = (s32[]{:T(128)}, bf16[4,512,4,64]{1,3,2,0:T(8,128)(2,1)S(1)}, bf16[4,2048,4,64]{1,3,2,0:T(8,128)(2,1)}, bf16[4,2048,4,64]{1,3,2,0:T(8,128)(2,1)}, bf...) while((s32[]{:T(128)}, ...), condition=%wide.region_12.13_spmd.clone, body=%wide.region_10.12_spmd.clone.sunk | while | flops 2748971008 | bytes 189340912 | solution.py:210
  508.9 9.3 fusion.142
  519.6 12.8 multiply_reduce_fusion.5
  532.3 15.8 multiply_convert_fusion.3
  548.2 6.8 fusion.143
  555.0 6.0 fusion.144
  566.7 9.3 fusion.142
  577.3 12.8 multiply_reduce_fusion.5
  590.1 15.8 multiply_convert_fusion.3
  605.9 6.8 fusion.143
  624.4 9.3 fusion.142
  635.1 12.8 multiply_reduce_fusion.5
  647.9 15.8 multiply_convert_fusion.3
  663.7 6.8 fusion.143
  682.2 9.3 fusion.142
  692.9 12.8 multiply_reduce_fusion.5
  705.7 15.8 multiply_convert_fusion.3
  721.5 6.8 fusion.143
  746.6 69.4 %reduce-scatter.9.cloned.1.call-done = bf16[512,1024]{0,1:T(8,128)(2,1)} async-done(((bf16[2048,1024]{0,1:T(8,128)(2,1)}), bf16[512,1024]{0,1:T(8,128)(2,1)}) %reduce-scatter.9.cloned.1.call-update) | async-done | bytes 1048592 | tf_op jit(solution)/shard_map/reduce_scatter | solution.py:217
  815.9 79.7 %reduce-scatter.7.cloned.1.call-done = bf16[512,1024]{0,1:T(8,128)(2,1)} async-done(((bf16[2048,1024]{0,1:T(8,128)(2,1)}), bf16[512,1024]{0,1:T(8,128)(2,1)}) %reduce-scatter.7.cloned.1.call-update) | async-done | bytes 1048592 | tf_op jit(solution)/shard_map/reduce_scatter | solution.py:214
  895.7 9.9 fusion.78
  907.2 10.6 fusion.83
  918.6 10.0 multiply_convert_fusion.1
  928.6 10.6 fusion.93
  939.8 10.3 add_convert_fusion.3
  950.1 6.7 fusion.85
  961.1 42.6 %all-reduce.17 = (f32[1024]{0:T(1024)S(1)}, f32[1024]{0:T(1024)S(1)}, f32[1024]{0:T(1024)S(1)}, f32[1024]{0:T(1024)S(1)}, f32[1024]{0:T(1024)S(1)}, /*index=5*/f...) all-reduce(f32[1024]{0:T(1024)S(1)} %get-tuple-element.160, ...), channel_id=4, replica_groups=mesh['grp'=8,'seq'=4] {'grp','seq'}, use_global_device_ids=true, to_apply=%region_18.19.clone | all-reduce | flops 12288 | bytes 98304
  1008.9 38.2 %reduce-scatter.13.cloned.1.call-done = f32[32,1024]{1,0:T(8,128)} async-done(((f32[1024,1024]{1,0:T(8,128)}), f32[32,1024]{1,0:T(8,128)}) %reduce-scatter.13.cloned.1.call-update) | async-done | bytes 131088 | tf_op jit(solution)/shard_map/reduce_scatter | solution.py:238
  1047.2 160.4 %reduce-scatter.11.cloned.1.call-done = f32[32,3072]{1,0:T(8,128)} async-done(((f32[1024,3072]{1,0:T(8,128)}), f32[32,3072]{1,0:T(8,128)}) %reduce-scatter.11.cloned.1.call-update) | async-done | bytes 393232 | tf_op jit(solution)/shard_map/reduce_scatter | solution.py:235
  1207.6 366.3 %reduce-scatter.15.cloned.1.call-done = f32[32,4096]{1,0:T(8,128)} async-done(((f32[1024,4096]{1,0:T(8,128)}), f32[32,4096]{1,0:T(8,128)}) %reduce-scatter.15.cloned.1.call-update) | async-done | bytes 524304 | tf_op jit(solution)/shard_map/reduce_scatter | solution.py:242
  1573.9 365.0 %reduce-scatter.17.cloned.1.call-done = f32[128,1024]{1,0:T(8,128)} async-done(((f32[4096,1024]{1,0:T(8,128)}), f32[128,1024]{1,0:T(8,128)}) %reduce-scatter.17.cloned.1.call-update) | async-done | bytes 524304 | tf_op jit(solution)/shard_map/reduce_scatter | solution.py:244
  (260 shorter events, 140.2 us)
Async XLA Ops:
  7.2 76.2 %all-gather.8.cloned.1.call-start = ((), (), s32[]{:S(2)}) async-start(), calls=%async_computation.6 | async-start | bytes 6488064 | tf_op jit(solution)/shard_map/all_gather | solution.py:115
  7.9 163.4 %all-gather.10.cloned.1.call-start = ((), (), s32[]{:S(2)}) async-start(), calls=%async_computation.7 | async-start | bytes 5242880 | tf_op jit(solution)/shard_map/all_gather | solution.py:152
  57.3 26.0 %copy-start.43 = (f32[1024]{0:T(1024)}, f32[1024]{0:T(1024)S(1)}, u32[]{:S(2)}) copy-start(f32[1024]{0:T(1024)S(1)} %convert_element_type.113) | copy-start | bytes 12292
  57.4 26.0 %copy-start.23 = (f32[1024]{0:T(1024)}, f32[1024]{0:T(1024)S(1)}, u32[]{:S(2)}) copy-start(f32[1024]{0:T(1024)S(1)} %convert_element_type.112) | copy-start | bytes 12292
  58.8 24.5 %copy-start.25 = (f32[512]{0:T(512)}, f32[512]{0:T(512)S(1)}, u32[]{:S(2)}) copy-start(f32[512]{0:T(512)S(1)} %broadcast_multiply_fusion.1) | copy-start | bytes 6148
  61.4 22.0 %copy-start.31 = (f32[512]{0:T(512)}, f32[512]{0:T(512)S(1)}, u32[]{:S(2)}) copy-start(f32[512]{0:T(512)S(1)} %fusion.76) | copy-start | bytes 6148
  90.0 73.5 %copy-start.19 = (s32[2048]{0:T(1024)S(1)}, s32[2048]{0:T(1024)}, u32[]{:S(2)}) copy-start(s32[2048]{0:T(1024)} %param.22) | copy-start | bytes 24580
  91.7 161.1 %all-gather.12.cloned.1.call-start = ((), (), s32[]{:S(2)}) async-start(), calls=%async_computation.8 | async-start | bytes 5242880 | tf_op jit(solution)/shard_map/all_gather | solution.py:151
  92.5 232.9 %all-gather.14.cloned.1.call-start = ((), (), s32[]{:S(2)}) async-start(), calls=%async_computation.9 | async-start | bytes 2162688 | tf_op jit(solution)/shard_map/all_gather | solution.py:118
  93.0 296.8 %all-gather.16.cloned.1.call-start = ((), (), s32[]{:S(2)}) async-start(), calls=%async_computation.10 | async-start | bytes 8650752 | tf_op jit(solution)/shard_map/all_gather | solution.py:122
  93.6 375.0 %all-gather.18.cloned.1.call-start = ((), (), s32[]{:S(2)}) async-start(), calls=%async_computation.11 | async-start | bytes 8650752 | tf_op jit(solution)/shard_map/all_gather | solution.py:124
  94.2 721.7 %reduce-scatter.9.cloned.1.call-start = ((), (), s32[]{:S(2)}) async-start(), calls=%async_computation.13 | async-start | bytes 5242880 | tf_op jit(solution)/shard_map/reduce_scatter | solution.py:217
  259.4 67.2 %copy-start = (bf16[512,1024]{1,0:T(8,128)(2,1)S(1)}, bf16[512,1024]{1,0:T(8,128)(2,1)}, u32[]{:S(2)}) copy-start(bf16[512,1024]{1,0:T(8,128)(2,1)} %param.20) | copy-start | bytes 3145732
  259.4 67.2 %copy-start.20 = (f32[1024]{0:T(1024)S(1)}, f32[1024]{0:T(1024)}, u32[]{:S(2)}) copy-start(f32[1024]{0:T(1024)} %convert_element_type.121) | copy-start | bytes 12292
  325.3 64.5 %copy-start.37 = (f32[1024]{0:T(1024)S(1)}, f32[1024]{0:T(1024)}, u32[]{:S(2)}) copy-start(f32[1024]{0:T(1024)} %convert_element_type.122) | copy-start | bytes 12292
  325.3 64.5 %copy-start.45 = (f32[1024]{0:T(1024)S(1)}, f32[1024]{0:T(1024)}, u32[]{:S(2)}) copy-start(f32[1024]{0:T(1024)} %convert_element_type.123) | copy-start | bytes 12292
  329.9 172.8 %copy-start.2 = (f32[512,1024]{1,0:T(8,128)}, f32[512,1024]{1,0:T(8,128)S(1)}, u32[]{:S(2)}) copy-start(f32[512,1024]{1,0:T(8,128)S(1)} %get-tuple-element.239) | copy-start | bytes 6291460
  330.0 172.8 %copy-start.29 = (f32[512]{0:T(512)}, f32[512]{0:T(512)S(1)}, u32[]{:S(2)}) copy-start(f32[512]{0:T(512)S(1)} %broadcast_multiply_fusion) | copy-start | bytes 6148
  330.3 172.4 %copy-start.39 = (f32[512]{0:T(512)}, f32[512]{0:T(512)S(1)}, u32[]{:S(2)}) copy-start(f32[512]{0:T(512)S(1)} %fusion.77) | copy-start | bytes 6148
  330.3 138.3 %copy-start.8 = (bf16[512,1024]{1,0:T(8,128)(2,1)S(1)}, bf16[512,1024]{1,0:T(8,128)(2,1)}, u32[]{:S(2)}) copy-start(bf16[512,1024]{1,0:T(8,128)(2,1)} %param.21) | copy-start | bytes 3145732
  330.3 138.3 %copy-start.21 = (f32[32,1,128]{2,1,0:T(1,128)S(1)}, f32[32,1,128]{2,1,0:T(1,128)}, u32[]{:S(2)}) copy-start(f32[32,1,128]{2,1,0:T(1,128)} %convert_element_type.143) | copy-start | bytes 49156
  468.6 28.6 %copy-start.49 = (bf16[1024,4096]{1,0:T(8,128)(2,1)S(1)}, bf16[1024,4096]{1,0:T(8,128)(2,1)}, u32[]{:S(2)}) copy-start(bf16[1024,4096]{1,0:T(8,128)(2,1)} %all-gather.16.cloned.1.call-done) | copy-start | bytes 25165828
  532.3 28.6 %slice-start = ((s8[16777216]{0:T(1024)(128)(4,1)}), s8[4194304]{0:T(1024)(128)(4,1)S(1)}, s32[]{:S(2)}) async-start(s8[16777216]{0:T(1024)(128)(4,1)} %bitcast.145), calls=%async_computation.18 | async-start | bytes 8388608 | tf_op jit(solution)/shard_map/while
  532.3 28.6 %slice-start.1 = ((s8[16777216]{0:T(1024)(128)(4,1)}), s8[4194304]{0:T(1024)(128)(4,1)S(1)}, s32[]{:S(2)}) async-start(s8[16777216]{0:T(1024)(128)(4,1)} %bitcast.145), calls=%async_computation.19 | async-start | bytes 8388608 | tf_op jit(solution)/shard_map/while
  532.3 28.6 %slice-start.2 = ((s8[16777216]{0:T(1024)(128)(4,1)}), s8[4194304]{0:T(1024)(128)(4,1)S(1)}, s32[]{:S(2)}) async-start(s8[16777216]{0:T(1024)(128)(4,1)} %bitcast.145), calls=%async_computation.20 | async-start | bytes 8388608 | tf_op jit(solution)/shard_map/while
  548.2 12.8 slice-start.3
  590.1 28.6 %slice-start = ((s8[16777216]{0:T(1024)(128)(4,1)}), s8[4194304]{0:T(1024)(128)(4,1)S(1)}, s32[]{:S(2)}) async-start(s8[16777216]{0:T(1024)(128)(4,1)} %bitcast.145), calls=%async_computation.18 | async-start | bytes 8388608 | tf_op jit(solution)/shard_map/while
  590.1 28.6 %slice-start.1 = ((s8[16777216]{0:T(1024)(128)(4,1)}), s8[4194304]{0:T(1024)(128)(4,1)S(1)}, s32[]{:S(2)}) async-start(s8[16777216]{0:T(1024)(128)(4,1)} %bitcast.145), calls=%async_computation.19 | async-start | bytes 8388608 | tf_op jit(solution)/shard_map/while
  590.1 28.6 %slice-start.2 = ((s8[16777216]{0:T(1024)(128)(4,1)}), s8[4194304]{0:T(1024)(128)(4,1)S(1)}, s32[]{:S(2)}) async-start(s8[16777216]{0:T(1024)(128)(4,1)} %bitcast.145), calls=%async_computation.20 | async-start | bytes 8388608 | tf_op jit(solution)/shard_map/while
  647.9 28.6 %slice-start = ((s8[16777216]{0:T(1024)(128)(4,1)}), s8[4194304]{0:T(1024)(128)(4,1)S(1)}, s32[]{:S(2)}) async-start(s8[16777216]{0:T(1024)(128)(4,1)} %bitcast.145), calls=%async_computation.18 | async-start | bytes 8388608 | tf_op jit(solution)/shard_map/while
  647.9 28.6 %slice-start.1 = ((s8[16777216]{0:T(1024)(128)(4,1)}), s8[4194304]{0:T(1024)(128)(4,1)S(1)}, s32[]{:S(2)}) async-start(s8[16777216]{0:T(1024)(128)(4,1)} %bitcast.145), calls=%async_computation.19 | async-start | bytes 8388608 | tf_op jit(solution)/shard_map/while
  647.9 28.6 %slice-start.2 = ((s8[16777216]{0:T(1024)(128)(4,1)}), s8[4194304]{0:T(1024)(128)(4,1)S(1)}, s32[]{:S(2)}) async-start(s8[16777216]{0:T(1024)(128)(4,1)} %bitcast.145), calls=%async_computation.20 | async-start | bytes 8388608 | tf_op jit(solution)/shard_map/while
  663.7 12.8 slice-start.3
  705.7 28.6 %slice-start = ((s8[16777216]{0:T(1024)(128)(4,1)}), s8[4194304]{0:T(1024)(128)(4,1)S(1)}, s32[]{:S(2)}) async-start(s8[16777216]{0:T(1024)(128)(4,1)} %bitcast.145), calls=%async_computation.18 | async-start | bytes 8388608 | tf_op jit(solution)/shard_map/while
  705.7 28.6 %slice-start.1 = ((s8[16777216]{0:T(1024)(128)(4,1)}), s8[4194304]{0:T(1024)(128)(4,1)S(1)}, s32[]{:S(2)}) async-start(s8[16777216]{0:T(1024)(128)(4,1)} %bitcast.145), calls=%async_computation.19 | async-start | bytes 8388608 | tf_op jit(solution)/shard_map/while
  705.7 28.6 %slice-start.2 = ((s8[16777216]{0:T(1024)(128)(4,1)}), s8[4194304]{0:T(1024)(128)(4,1)S(1)}, s32[]{:S(2)}) async-start(s8[16777216]{0:T(1024)(128)(4,1)} %bitcast.145), calls=%async_computation.20 | async-start | bytes 8388608 | tf_op jit(solution)/shard_map/while
  721.5 12.8 slice-start.3
  740.4 155.2 %copy-start.11 = (bf16[4,512,4,64]{1,3,2,0:T(8,128)(2,1)}, bf16[4,512,4,64]{1,3,2,0:T(8,128)(2,1)S(1)}, u32[]{:S(2)}) copy-start(bf16[4,512,4,64]{1,3,2,0:T(8,128)(2,1)S(1)} %get-tuple-element.109) | copy-start | bytes 3145732
  740.4 155.2 %reduce-scatter.7.cloned.1.call-start = ((), (), s32[]{:S(2)}) async-start(), calls=%async_computation.12 | async-start | bytes 5242880 | tf_op jit(solution)/shard_map/reduce_scatter | solution.py:214
  741.2 154.4 %copy-start.1 = (bf16[512,1024]{1,0:T(8,128)(2,1)S(1)}, bf16[512,1024]{1,0:T(8,128)(2,1)}, u32[]{:S(2)}) copy-start(bf16[512,1024]{1,0:T(8,128)(2,1)} %param.20) | copy-start | bytes 3145732
  741.2 154.4 %copy-start.24 = (f32[1024]{0:T(1024)S(1)}, f32[1024]{0:T(1024)}, u32[]{:S(2)}) copy-start(f32[1024]{0:T(1024)} %copy-done.23) | copy-start | bytes 12292
  741.2 154.4 %copy-start.26 = (f32[512]{0:T(512)S(1)}, f32[512]{0:T(512)}, u32[]{:S(2)}) copy-start(f32[512]{0:T(512)} %copy-done.25) | copy-start | bytes 6148
  741.2 154.4 %copy-start.32 = (f32[512]{0:T(512)S(1)}, f32[512]{0:T(512)}, u32[]{:S(2)}) copy-start(f32[512]{0:T(512)} %copy-done.31) | copy-start | bytes 6148
  741.2 154.4 %copy-start.44 = (f32[1024]{0:T(1024)S(1)}, f32[1024]{0:T(1024)}, u32[]{:S(2)}) copy-start(f32[1024]{0:T(1024)} %copy-done.43) | copy-start | bytes 12292
  741.2 305.9 %reduce-scatter.13.cloned.1.call-start = ((), (), s32[]{:S(2)}) async-start(), calls=%async_computation.15 | async-start | bytes 4325376 | tf_op jit(solution)/shard_map/reduce_scatter | solution.py:238
  746.5 461.1 %reduce-scatter.11.cloned.1.call-start = ((), (), s32[]{:S(2)}) async-start(), calls=%async_computation.14 | async-start | bytes 12976128 | tf_op jit(solution)/shard_map/reduce_scatter | solution.py:235
  905.7 668.3 %reduce-scatter.15.cloned.1.call-start = ((), (), s32[]{:S(2)}) async-start(), calls=%async_computation.16 | async-start | bytes 17301504 | tf_op jit(solution)/shard_map/reduce_scatter | solution.py:242
  917.9 1021.1 %reduce-scatter.17.cloned.1.call-start = ((), (), s32[]{:S(2)}) async-start(), calls=%async_computation.17 | async-start | bytes 17301504 | tf_op jit(solution)/shard_map/reduce_scatter | solution.py:244
  (31 other events, 119.3 us)
Sparse Core Ops, SparseCore 0:
  10.9 72.3 all-gather.7
  91.8 79.4 all-gather.9
  173.5 79.3 all-gather.11
  255.6 55.0 all-gather.13
  313.5 76.2 all-gather.15
  392.6 75.9 all-gather.17
  740.6 75.3 reduce-scatter.8
  818.3 77.2 reduce-scatter.6
  898.5 148.6 reduce-scatter.12
  1053.6 153.9 reduce-scatter.10
  1210.6 363.3 reduce-scatter.14
  1576.8 362.1 reduce-scatter.16
where the time goes:
time: 1950 us
  waiting for transfers between devices  1310 us (67%)
  matrix products  314 us (16%)
  blocking collectives  152 us (8%)
  other arithmetic  110 us (6%)
  local copies, waits for them, and re-layouts  38.5 us (2%)
    reduce_scatter x1, waiting for transfers between devices, per_device(): lax.psum_scatter(up_grad, ('grp', 'seq'), scatter_dimension=0, tiled=True)  366 us
    reduce_scatter x1, waiting for transfers between devices, per_device(): lax.psum_scatter(down_grad, ('grp', 'seq'), scatter_dimension=0, tiled=True)  365 us
    reduce_scatter x1, waiting for transfers between devices, per_device(): lax.psum_scatter(joint_grad, ('grp', 'seq'), scatter_dimension=0, tiled=T...  160 us
    unnamed x2, blocking collectives  85.3 us
    reduce_scatter x1, waiting for transfers between devices, per_device(): lax.psum_scatter(join_heads(grad_k_parts).astype(jnp.bfloat16), 'seq', sc...  79.7 us
    all_gather x1, waiting for transfers between devices, per_device(): lax.all_gather(keys, 'seq', axis=0, tiled=True)  75 us
    reduce_scatter x1, waiting for transfers between devices, per_device(): lax.psum_scatter(join_heads(grad_v_parts).astype(jnp.bfloat16), 'seq', sc...  69.4 us
    all_gather x1, waiting for transfers between devices, per_device(): lax.all_gather(down_weight, ('grp', 'seq'), axis=0, tiled=True)  68.5 us
  transfers between devices with their start and end apart: 12, of which 11 were waited for; matrix products, arithmetic and copies ran while one was open for 9% of the time, Pallas kernels for 0%

commit v1 on v0

v1 whole, which is shorter than its diff:
```python
from functools import partial
import math

import jax
import jax.numpy as jnp
from jax import lax
from jax.experimental import pallas as pl
from jax.experimental.pallas import tpu as pltpu
from jax.sharding import PartitionSpec as P

HEADS = 16


EPS = 1e-06
MASKED = -1e30


def layer_norm(value, gain, shift):
    center = value - jnp.mean(value, axis=-1, keepdims=True)
    spread = jnp.mean(center * center, axis=-1, keepdims=True)
    return center * lax.rsqrt(spread + EPS) * gain + shift


def scaled_norm(value, gain):
    return layer_norm(value, gain, 0.0)


def rows_dot(left, right):
    return lax.dot_general(
        left, right, (((0,), (0,)), ((), ())), preferred_element_type=jnp.float32
    )


def dot_back(left, right):
    return lax.dot_general(
        left, right, (((1,), (1,)), ((), ())), preferred_element_type=jnp.float32
    )


BLOCK = 256


def head_lanes(shape, head, size):
    lane = lax.broadcasted_iota(jnp.int32, shape, len(shape) - 1)
    return lane // size == head


def forward_kernel(heads, first_ref, last_ref, q_ref, kv_ref, row_ref, col_ref, out_ref, lse_ref, s_ref):
    step = pl.program_id(0)
    first = first_ref[step]
    last = last_ref[step]
    width = q_ref.shape[1]
    size = width // heads
    query = q_ref[...] * (1.0 / math.sqrt(size))
    mine = row_ref[...]
    for head in range(heads):
        own = jnp.where(head_lanes(query.shape, head, size), query, jnp.zeros_like(query))

        def scores_at(at, peak):
            rows = pl.ds(pl.multiple_of(at * BLOCK, BLOCK), BLOCK)
            scores = lax.dot_general(
                own,
                kv_ref[rows, :width],
                (((1,), (1,)), ((), ())),
                preferred_element_type=jnp.float32,
            )
            scores = jnp.where(mine == col_ref[at], scores, MASKED)
            s_ref[head, at] = scores
            return jnp.maximum(peak, scores)

        peak = lax.fori_loop(first, last, scores_at, jnp.full((BLOCK, BLOCK), MASKED, jnp.float32))
        peak = jnp.max(peak, axis=-1, keepdims=True)

        def sum_at(at, carry):
            total, result = carry
            rows = pl.ds(pl.multiple_of(at * BLOCK, BLOCK), BLOCK)
            expo = jnp.exp(s_ref[head, at] - peak)
            result = result + jnp.dot(
                expo.astype(jnp.bfloat16),
                kv_ref[rows, width:],
                preferred_element_type=jnp.float32,
            )
            return (total + expo, result)

        total, result = lax.fori_loop(
            first,
            last,
            sum_at,
            (jnp.zeros((BLOCK, BLOCK), jnp.float32), jnp.zeros((BLOCK, width), jnp.float32)),
        )
        total = jnp.sum(total, axis=-1, keepdims=True)
        result = result / total
        lse_ref[:, head : head + 1] = peak + jnp.log(total)
        if head == 0:
            merged = result
        else:
            merged = jnp.where(head_lanes(result.shape, head, size), result, merged)
    out_ref[...] = merged.astype(out_ref.dtype)


def backward_kernel(
    heads, first_ref, last_ref, q_ref, kv_ref, g_ref, lse_ref, delta_ref, row_ref, col_ref,
    dq_ref, dkv_ref, sum_ref
):
    step = pl.program_id(0)
    first = first_ref[step]
    last = last_ref[step]
    width = q_ref.shape[1]
    size = width // heads
    scale = 1.0 / math.sqrt(size)

    @pl.when(step == 0)
    def clear():
        sum_ref[...] = jnp.zeros_like(sum_ref)

    keys = kv_ref[:, :width] * scale
    values = kv_ref[:, width:]
    mine = row_ref[...]
    for head in range(heads):
        lanes = head_lanes(keys.shape, head, size)
        own_keys = jnp.where(lanes, keys, jnp.zeros_like(keys))
        own_values = jnp.where(lanes, values, jnp.zeros_like(values))

        def at_queries(at, carry):
            grad_keys, grad_values = carry
            rows = pl.ds(pl.multiple_of(at * BLOCK, BLOCK), BLOCK)
            query = q_ref[rows, :]
            grad = g_ref[rows, :]
            scores = lax.dot_general(
                own_keys, query, (((1,), (1,)), ((), ())), preferred_element_type=jnp.float32
            )
            scores = jnp.where(mine == col_ref[at], scores, MASKED)
            weights = jnp.exp(scores - lse_ref[at, head : head + 1, :])
            grad_probs = lax.dot_general(
                own_values, grad, (((1,), (1,)), ((), ())), preferred_element_type=jnp.float32
            )
            grad_scores = (weights * (grad_probs - delta_ref[at, head : head + 1, :])).astype(
                jnp.bfloat16
            )
            grad_values = grad_values + jnp.dot(
                weights.astype(jnp.bfloat16), grad, preferred_element_type=jnp.float32
            )
            grad_keys = grad_keys + jnp.dot(
                grad_scores, query, preferred_element_type=jnp.float32
            )
            sum_ref[rows, :] += rows_dot(grad_scores, own_keys)
            return (grad_keys, grad_values)

        zero = jnp.zeros((BLOCK, width), jnp.float32)
        grad_keys, grad_values = lax.fori_loop(first, last, at_queries, (zero, zero))
        if head == 0:
            merged_keys, merged_values = grad_keys, grad_values
        else:
            merged_keys = jnp.where(lanes, grad_keys, merged_keys)
            merged_values = jnp.where(lanes, grad_values, merged_values)
    dkv_ref[:, :width] = (merged_keys * scale).astype(jnp.bfloat16)
    dkv_ref[:, width:] = merged_values.astype(jnp.bfloat16)

    @pl.when(step == pl.num_programs(0) - 1)
    def store():
        dq_ref[...] = sum_ref[...].astype(jnp.bfloat16)


def whole(shape):
    return pl.BlockSpec(shape, lambda step, first, last: (0,) * len(shape))


def by_rows(width):
    return pl.BlockSpec((BLOCK, width), lambda step, first, last: (step, 0))


def block_bounds(labels):
    per_block = labels.reshape(-1, BLOCK)
    least, most = per_block[:, 0], per_block[:, -1]
    first = jnp.sum(labels[None, :] < least[:, None], axis=1) // BLOCK
    last = (jnp.sum(labels[None, :] <= most[:, None], axis=1) + BLOCK - 1) // BLOCK
    return first.astype(jnp.int32), last.astype(jnp.int32)


def attend(joint, labels, bounds, heads):
    count, width = joint.shape[0], joint.shape[1] // 3
    blocks = count // BLOCK
    return pl.pallas_call(
        partial(forward_kernel, heads),
        grid_spec=pltpu.PrefetchScalarGridSpec(
            num_scalar_prefetch=2,
            grid=(blocks,),
            in_specs=[
                by_rows(width),
                whole((count, 2 * width)),
                by_rows(1),
                whole((blocks, 1, BLOCK)),
            ],
            out_specs=[by_rows(width), by_rows(heads)],
            scratch_shapes=[pltpu.VMEM((heads, blocks, BLOCK, BLOCK), jnp.float32)],
        ),
        out_shape=[
            jax.ShapeDtypeStruct((count, width), jnp.bfloat16),
            jax.ShapeDtypeStruct((count, heads), jnp.float32),
        ],
        name="attend",
    )(
        *bounds,
        joint[:, :width],
        joint[:, width:],
        labels.reshape(count, 1),
        labels.reshape(blocks, 1, BLOCK),
    )


def attend_back(joint, grad, spread, inner, labels, bounds, heads):
    count, width = joint.shape[0], joint.shape[1] // 3
    blocks = count // BLOCK

    def in_rows(value):
        return value.reshape(blocks, BLOCK, heads).transpose(0, 2, 1)

    return pl.pallas_call(
        partial(backward_kernel, heads),
        grid_spec=pltpu.PrefetchScalarGridSpec(
            num_scalar_prefetch=2,
            grid=(blocks,),
            in_specs=[
                whole((count, width)),
                by_rows(2 * width),
                whole((count, width)),
                whole((blocks, heads, BLOCK)),
                whole((blocks, heads, BLOCK)),
                by_rows(1),
                whole((blocks, 1, BLOCK)),
            ],
            out_specs=[whole((count, width)), by_rows(2 * width)],
            scratch_shapes=[pltpu.VMEM((count, width), jnp.float32)],
        ),
        out_shape=[
            jax.ShapeDtypeStruct((count, width), jnp.bfloat16),
            jax.ShapeDtypeStruct((count, 2 * width), jnp.bfloat16),
        ],
        name="attend_back",
    )(
        *bounds,
        joint[:, :width],
        joint[:, width:],
        grad,
        in_rows(spread),
        in_rows(inner),
        labels.reshape(count, 1),
        labels.reshape(blocks, 1, BLOCK),
    )


def to_heads(rows, parts, seq):
    count, width = rows.shape
    share = width // parts // seq
    split = rows.reshape(count, parts, seq, share).transpose(2, 0, 1, 3)
    moved = lax.all_to_all(split.reshape(seq, count, parts * share), "seq", 0, 0)
    return moved.reshape(seq * count, parts * share)


def to_rows(rows, parts, seq):
    count, width = rows.shape
    share = width // parts
    moved = lax.all_to_all(rows.reshape(seq, count // seq, width), "seq", 0, 0)
    split = moved.reshape(seq, count // seq, parts, share).transpose(1, 2, 0, 3)
    return split.reshape(count // seq, parts * seq * share)


def scatter_sum(value):
    near = lax.psum_scatter(value.astype(jnp.bfloat16), "grp", scatter_dimension=0, tiled=True)
    return lax.psum_scatter(near, "seq", scatter_dimension=0, tiled=True).astype(jnp.float32)


def per_device(
    tokens,
    cotangent,
    image_of_token,
    ln1_gain,
    ln1_bias,
    qkv_weight,
    q_bias,
    v_bias,
    out_weight,
    out_bias,
    ln2_gain,
    ln2_bias,
    up_weight,
    up_bias,
    down_weight,
    down_bias,
):
    f32 = jnp.float32
    bf16 = jnp.bfloat16
    width = tokens.shape[1]
    gathered = (
        lax.all_gather(ln1_gain, ("grp", "seq"), axis=0, tiled=True),
        lax.all_gather(ln1_bias, ("grp", "seq"), axis=0, tiled=True),
        lax.all_gather(qkv_weight, ("grp", "seq"), axis=0, tiled=True),
        lax.all_gather(q_bias, ("grp", "seq"), axis=0, tiled=True),
        lax.all_gather(v_bias, ("grp", "seq"), axis=0, tiled=True),
        lax.all_gather(out_weight, ("grp", "seq"), axis=0, tiled=True),
        lax.all_gather(out_bias, ("grp", "seq"), axis=0, tiled=True),
        lax.all_gather(ln2_gain, ("grp", "seq"), axis=0, tiled=True),
        lax.all_gather(ln2_bias, ("grp", "seq"), axis=0, tiled=True),
        lax.all_gather(up_weight, ("grp", "seq"), axis=0, tiled=True),
        lax.all_gather(up_bias, ("grp", "seq"), axis=0, tiled=True),
        lax.all_gather(down_weight, ("grp", "seq"), axis=0, tiled=True),
        lax.all_gather(down_bias, ("grp", "seq"), axis=0, tiled=True),
    )
    (
        gain_first,
        shift_first,
        w_joint,
        bias_query,
        bias_value,
        w_out,
        bias_out,
        gain_second,
        shift_second,
        w_up,
        bias_up,
        w_down,
        bias_down,
    ) = gathered
    inputs = tokens.astype(f32)
    normed_first = layer_norm(inputs, gain_first.astype(f32), shift_first.astype(f32)).astype(bf16)
    zeros = jnp.zeros((width,), f32)
    joint_bias = jnp.concatenate([bias_query.astype(f32), zeros, bias_value.astype(f32)])
    joint = (jnp.dot(normed_first, w_joint, preferred_element_type=f32) + joint_bias).astype(bf16)
    seq = lax.axis_size("seq")
    heads = HEADS // seq
    bounds = block_bounds(image_of_token)
    own_joint = to_heads(joint, 3, seq)
    own_attended, spread = attend(own_joint, image_of_token, bounds, heads)
    attended = to_rows(own_attended, 1, seq)
    resid = inputs + jnp.dot(attended, w_out, preferred_element_type=f32) + bias_out.astype(f32)
    normed_second = layer_norm(resid, gain_second.astype(f32), shift_second.astype(f32)).astype(
        bf16
    )
    hidden = jnp.dot(normed_second, w_up, preferred_element_type=f32) + bias_up.astype(f32)
    active = jax.nn.gelu(hidden, approximate=False).astype(bf16)
    output = (
        resid + jnp.dot(active, w_down, preferred_element_type=f32) + bias_down.astype(f32)
    ).astype(bf16)
    down_grad = rows_dot(active, cotangent).astype(bf16)
    down_bias_grad = jnp.sum(cotangent.astype(f32), axis=0)
    grad_active = dot_back(cotangent, w_down)
    _, gelu_back = jax.vjp(partial(jax.nn.gelu, approximate=False), hidden)
    grad_hidden = gelu_back(grad_active)[0].astype(bf16)
    up_grad = rows_dot(normed_second, grad_hidden).astype(bf16)
    grad_hidden, down_grad, up_grad = lax.optimization_barrier((grad_hidden, down_grad, up_grad))
    down_grad = scatter_sum(down_grad)
    up_grad = scatter_sum(up_grad)
    up_bias_grad = jnp.sum(grad_hidden.astype(f32), axis=0)
    grad_normed = dot_back(grad_hidden, w_up)
    _, second_back = jax.vjp(scaled_norm, resid, gain_second.astype(f32))
    grad_through, gain_second_grad = second_back(grad_normed)
    shift_second_grad = jnp.sum(grad_normed, axis=0)
    grad_resid = cotangent.astype(f32) + grad_through
    grad_branch = grad_resid.astype(bf16)
    out_grad = rows_dot(attended, grad_branch).astype(bf16)
    grad_branch, out_grad = lax.optimization_barrier((grad_branch, out_grad))
    out_grad = scatter_sum(out_grad)
    out_bias_grad = jnp.sum(grad_branch.astype(f32), axis=0)
    grad_attended = dot_back(grad_branch, w_out).astype(bf16)
    own_grad = to_heads(grad_attended, 1, seq)
    inner = jnp.sum(
        (own_grad.astype(f32) * own_attended.astype(f32)).reshape(own_grad.shape[0], heads, -1),
        axis=-1,
    )
    grad_q, grad_kv = attend_back(
        own_joint, own_grad, spread, inner, image_of_token, bounds, heads
    )
    grad_joint = to_rows(jnp.concatenate([grad_q, grad_kv], axis=1), 3, seq)
    joint_grad = scatter_sum(rows_dot(normed_first, grad_joint))
    column_sums = jnp.sum(grad_joint.astype(f32), axis=0)
    query_bias_grad = column_sums[:width]
    value_bias_grad = column_sums[2 * width :]
    grad_first = dot_back(grad_joint, w_joint)
    _, first_back = jax.vjp(scaled_norm, inputs, gain_first.astype(f32))
    grad_entry, gain_first_grad = first_back(grad_first)
    shift_first_grad = jnp.sum(grad_first, axis=0)
    input_grad = (grad_resid + grad_entry).astype(bf16)
    summed = (
        lax.psum_scatter(gain_first_grad, ("grp", "seq"), scatter_dimension=0, tiled=True),
        lax.psum_scatter(shift_first_grad, ("grp", "seq"), scatter_dimension=0, tiled=True),
        joint_grad,
        lax.psum_scatter(query_bias_grad, ("grp", "seq"), scatter_dimension=0, tiled=True),
        lax.psum_scatter(value_bias_grad, ("grp", "seq"), scatter_dimension=0, tiled=True),
        out_grad,
        lax.psum_scatter(out_bias_grad, ("grp", "seq"), scatter_dimension=0, tiled=True),
        lax.psum_scatter(gain_second_grad, ("grp", "seq"), scatter_dimension=0, tiled=True),
        lax.psum_scatter(shift_second_grad, ("grp", "seq"), scatter_dimension=0, tiled=True),
        up_grad,
        lax.psum_scatter(up_bias_grad, ("grp", "seq"), scatter_dimension=0, tiled=True),
        down_grad,
        lax.psum_scatter(down_bias_grad, ("grp", "seq"), scatter_dimension=0, tiled=True),
    )
    return (output, input_grad) + tuple(summed)


def solution(mesh):
    placed = (
        P(("grp", "seq"), None),
        P(("grp", "seq"), None),
        P("grp"),
        P(("grp", "seq")),
        P(("grp", "seq")),
        P(("grp", "seq"), None),
        P(("grp", "seq")),
        P(("grp", "seq")),
        P(("grp", "seq"), None),
        P(("grp", "seq")),
        P(("grp", "seq")),
        P(("grp", "seq")),
        P(("grp", "seq"), None),
        P(("grp", "seq")),
        P(("grp", "seq"), None),
        P(("grp", "seq")),
    )
    return jax.shard_map(
        per_device,
        mesh=mesh,
        in_specs=placed,
        out_specs=(
            P(("grp", "seq"), None),
            P(("grp", "seq"), None),
            P(("grp", "seq")),
            P(("grp", "seq")),
            P(("grp", "seq"), None),
            P(("grp", "seq")),
            P(("grp", "seq")),
            P(("grp", "seq"), None),
            P(("grp", "seq")),
            P(("grp", "seq")),
            P(("grp", "seq")),
            P(("grp", "seq"), None),
            P(("grp", "seq")),
            P(("grp", "seq"), None),
            P(("grp", "seq")),
        ),
        check_vma=False,
    )
```

time: 1950 us -> 827 us (0.42)
  waiting for transfers between devices: 1310 us -> 281 us
  matrix products: 314 us -> 107 us
  Pallas kernels: 0 us -> 135 us
  other arithmetic: 110 us -> 38.3 us
  blocking collectives: 152 us -> 180 us
    reduce_scatter x6 -> x8, waiting for transfers between devices: 1080 us -> 90.3 us  [the longest x4 53 us: scatter_sum(): lax.psum_scatter(value.astype(jnp.bfloat16), 'grp', scatter_dimension=0,...]
    dot_general x28 -> x0, matrix products: 205 us -> none  [the longest x8 55.2 us: block_scores(): jnp.einsum('qhd,khd->hqk', query, keys, preferred_element_type=jnp.float32)]
    all_to_all x0 -> x4, waiting for transfers between devices: none -> 165 us  [the longest x2 98.1 us: to_heads(): lax.all_to_all(split.reshape(seq, count, parts * share), 'seq', 0, 0)]
    pallas_call x0 -> x2, Pallas kernels: none -> 135 us  [the longest x1 67.9 us: attend_back(): pl.pallas_call(partial(backward_kernel, heads), grid_spec=pltpu.PrefetchS...]
    all_gather x2 -> x0, waiting for transfers between devices: 82.2 us -> none  [the longest x1 75 us: per_device(): lax.all_gather(keys, 'seq', axis=0, tiled=True)]
    all_gather x1, waiting for transfers between devices: 68.5 us -> 0.01 us  [per_device(): lax.all_gather(down_weight, ('grp', 'seq'), axis=0, tiled=True)]
    all_gather x1, waiting for transfers between devices: 59.4 us -> 0.02 us  [per_device(): lax.all_gather(up_weight, ('grp', 'seq'), axis=0, tiled=True)]
    convert_element_type x4 -> x5, other arithmetic: 63.3 us -> 7.1 us  [the longest x4 6.77 us: scatter_sum(): lax.psum_scatter(near, 'seq', scatter_dimension=0, tiled=True)]
  transfers between devices with their start and end apart: 12 -> 16, of which waited for: 11 -> 8; matrix products, arithmetic and copies ran while one was open for 9% -> 14% of each run, Pallas kernels for 0% -> 16%
where the time goes in v1:
time: 827 us; the launch traced here: 821 us
  waiting for transfers between devices  281 us (34%)
  blocking collectives  180 us (22%)
  Pallas kernels  135 us (16%)
  matrix products  107 us (13%)
  local copies, waits for them, and re-layouts  48.8 us (6%)
  other arithmetic  38.3 us (5%)
  starting transfers between devices  15.5 us (2%)
  between operations  15.2 us (2%)
    all_to_all x2, waiting for transfers between devices, to_heads(): lax.all_to_all(split.reshape(seq, count, parts * share), 'seq', 0, 0)  98.1 us
    all_gather x1, blocking collectives, per_device(): lax.all_gather(up_bias, ('grp', 'seq'), axis=0, tiled=True)  96.6 us
    unnamed x2, blocking collectives  83.7 us
    pallas_call x1, Pallas kernels, attend_back(): pl.pallas_call(partial(backward_kernel, heads), grid_spec=pltpu.PrefetchS...  67.9 us
    all_to_all x2, waiting for transfers between devices, to_rows(): moved = lax.all_to_all(rows.reshape(seq, count // seq, width), 'seq', 0, 0)  67 us
    pallas_call x1, Pallas kernels, attend(): pl.pallas_call(partial(forward_kernel, heads), grid_spec=pltpu.PrefetchSc...  66.9 us
    reduce_scatter x4, waiting for transfers between devices, scatter_sum(): lax.psum_scatter(value.astype(jnp.bfloat16), 'grp', scatter_dimension=0,...  53 us
    dot_general x4, matrix products, dot_back(): lax.dot_general(left, right, (((1,), (1,)), ((), ())), preferred_element_...  47.2 us
  transfers between devices with their start and end apart: 16, of which 8 were waited for; matrix products, arithmetic and copies ran while one was open for 14% of the time, Pallas kernels for 16%

profile of v1, /device:TPU:0, one launch (start us, length us, event | category | flops | bytes accessed | tf_op | source)
XLA Modules:
  0.0 821.2 jit_solution(7861542057104341653)
XLA Ops:
  16.7 42.4 %all-reduce.18 = (bf16[1024]{0:T(1024)(128)(2,1)S(1)}, bf16[1024]{0:T(1024)(128)(2,1)S(1)}, bf16[1024]{0:T(1024)(128)(2,1)S(1)}, bf16[1024]{0:T(1024)(128)(2,1)S...) all-reduce(bf16[1024]{0:T(1024)(128)(2,1)S(1)} %dynamic-update-slic, ...), channel_id=1, replica_groups=mesh['grp'=8,'seq'=4] {'grp','seq'}, use_global_device_ids=true, to_apply=%add.3 | all-reduce | flops 8192 | bytes 32768
  62.9 20.4 %all-gather.6.cloned.1.call-done = bf16[1024,3072]{1,0:T(8,128)(2,1)} async-done(((bf16[32,3072]{1,0:T(8,128)(2,1)}), bf16[1024,3072]{1,0:T(8,128)(2,1)}) %all-gather.6.cloned.1.call-update) | async-done | bytes 6291472 | tf_op jit(solution)/shard_map/all_gather | solution.py:297
  83.3 8.4 %add_convert_fusion.1 = bf16[512,3072]{1,0:T(8,128)(2,1)} fusion(bf16[1024,3072]{1,0:T(8,128)(2,1)} %all-gather.6.cloned.1.call-done, f32[3072]{0:T(1024)S(1)} %pad_maximum_fusion.1, bf16[512,1024]{1,0:T(8,128)(2,1)} %param.16, f32[1024]{0:T(1024)S(1)} %convert_element_type.113, f32[1024]{0:T(1024)S(1)} %convert_element_type.112, f32[512]{0:T(512)S(1)} %fusion.19, ...), kind=kOutput, calls=%fused_computation.21 | convolution fusion | flops 3227516928 | bytes 10510336 | tf_op jit(solution)/shard_map/dot_general | solution.py:328
  91.7 5.5 reshape.153
  97.2 4.3 copy.69
  101.6 3.8 all-to-all-start
  107.7 77.6 %all-to-all-done = bf16[4,512,768]{1,2,0:T(8,128)(2,1)S(1)} async-done(((bf16[4,512,768]{1,2,0:T(8,128)(2,1)}), bf16[4,512,768]{1,2,0:T(8,128)(2,1)S(1)}, u32[]{:S(2)}, u32[]{:S(2)}) %all-to-all-start) | async-done | bytes 3145760 | tf_op jit(solution)/shard_map/all_to_all | solution.py:256
  185.3 2.8 copy.70
  188.1 2.3 slice.36.q_ref
  190.4 3.1 slice.37.kv_ref
  193.5 66.9 %attend.1 = (bf16[2048,256]{1,0:T(8,128)(2,1)}, f32[2048,4]{1,0:T(8,128)}) custom-call(s32[8]{0:T(128)} %get-tuple-element.74.first_ref, s32[8]{0:T(128)} %get-tuple-element.73.last_ref, bf16[2048,256]{1,0:T(8,128)(2,1)} %slice.36.q_ref, bf16[2048,512]{1,0:T(8,128)(2,1)} %slice.37.kv_ref, s32[2048,1]{1,0:T(8,128)} %copy.71.row_ref, s32[8,1,256]{2,1,0:T(1,128)} %bitcast.68), custom_call_target="tpu_custom_call" | custom-call | tf_op jit(solution)/shard_map/attend/pallas_call | solution.py:183
  260.4 2.4 copy.72
  262.8 3.5 all-to-all-start.1
  266.4 96.6 %all-gather = bf16[32,1,128]{2,1,0:T(2,128)(2,1)S(1)} all-gather(bf16[1,1,128]{2,1,0:T(2,128)(2,1)S(1)} %bitcast.77), channel_id=1, replica_groups=mesh['grp'=8,'seq'=4] {'grp','seq'}, dimensions={0}, use_global_device_ids=true | all-gather | bytes 8448 | tf_op jit(solution)/shard_map/all_gather | solution.py:305
  364.1 3.3 fusion.29
  367.8 10.7 %fusion.24 = f32[512,4096]{1,0:T(8,128)} fusion(bf16[1024,4096]{1,0:T(8,128)(2,1)} %all-gather.10.cloned.1.call-done, f32[512,1024]{1,0:T(8,128)S(1)} %get-tuple-element.70, f32[1024]{0:T(1024)S(1)} %convert_element_type.120, f32[1024]{0:T(1024)S(1)} %convert_element_type.119, f32[512]{0:T(512)S(1)} %fusion.20, f32[512]{0:T(512)S(1)} %broadcast_multiply_fusion), kind=kOutput, calls=%fused_computation.80 | convolution fusion | flops 4297588736 | bytes 18886656 | tf_op jit(solution)/shard_map/dot_general | solution.py:339
  378.5 27.3 %add_convert_fusion = (bf16[512,4096]{1,0:T(8,128)(2,1)}, f32[512,4096]{1,0:T(8,128)}) fusion(f32[512,4096]{1,0:T(8,128)} %fusion.24, f32[4096]{0:T(1024)S(1)} %bitcast.73, bf16[512,1024]{1,0:T(8,128)(2,1)S(1)} %copy-done.11, bf16[4096,1024]{1,0:T(8,128)(2,1)} %all-gather.12.cloned.1.call-done), kind=kOutput, calls=%fused_computation.3 | convolution fusion | flops 4448059392 | bytes 30425088 | tf_op jit(solution)/shard_map/dot_general | solution.py:35
  405.8 9.8 %multiply_convert_fusion = bf16[512,4096]{1,0:T(8,128)(2,1)} fusion(f32[512,4096]{1,0:T(8,128)} %get-tuple-element.64, f32[512,4096]{1,0:T(8,128)} %fusion.24, f32[4096]{0:T(1024)S(1)} %bitcast.74), kind=kLoop, calls=%fused_computation.4 | loop fusion | flops 8388608 | bytes 20987904 | tf_op jit(solution)/shard_map/convert_element_type | solution.py:340
  415.6 9.2 %convolution_convert_fusion.1 = bf16[4096,1024]{1,0:T(8,128)(2,1)} fusion(bf16[512,4096]{1,0:T(8,128)(2,1)} %multiply_convert_fusion, bf16[512,1024]{1,0:T(8,128)(2,1)S(1)} %copy-done.11), kind=kOutput, calls=%fused_computation.19 | convolution fusion | flops 4299161600 | bytes 13631488 | tf_op jit(solution)/shard_map/dot_general | solution.py:29
  424.8 9.2 %convolution_convert_fusion = bf16[1024,4096]{1,0:T(8,128)(2,1)} fusion(bf16[512,4096]{1,0:T(8,128)(2,1)} %get-tuple-element.25, f32[512,1024]{1,0:T(8,128)S(1)} %get-tuple-element.70, f32[1024]{0:T(1024)S(1)} %convert_element_type.120, f32[1024]{0:T(1024)S(1)} %convert_element_type.119, f32[512]{0:T(512)S(1)} %fusion.20, f32[512]{0:T(512)S(1)} %broadcast_multiply_fusion), kind=kOutput, calls=%fused_computation.18 | convolution fusion | flops 4301783040 | bytes 14692352 | tf_op jit(solution)/shard_map/dot_general | solution.py:29
  434.0 8.7 %multiply_reduce_fusion = (f32[1024]{0:T(1024)S(1)}, f32[512]{0:T(512)S(1)}, f32[1024]{0:T(1024)S(1)}, f32[512,1024]{1,0:T(8,128)S(1)}) fusion(f32[512,1024]{1,0:T(8,128)S(1)} %get-tuple-element.70, f32[512]{0:T(512)S(1)} %fusion.20, f32[512]{0:T(512)S(1)} %broadcast_multiply_fusion, f32[1024]{0:T(1024)S(1)} %convert_element_type.119, ...), kind=kOutput, calls=%fused_computation.44 | convolution fusion | flops 4299159040 | bytes 16795648 | tf_op jit(solution)/shard_map/dot_general | solution.py:35
  445.4 2.7 convolution_convert_fusion.3
  450.3 2.3 convolution_convert_fusion.4
  452.5 1.9 reshape.161
  455.6 3.7 all-to-all-start.2
  460.3 20.5 %all-to-all-done.2 = bf16[4,512,256]{2,1,0:T(8,128)(2,1)S(1)} async-done(((bf16[4,512,256]{2,1,0:T(8,128)(2,1)}), bf16[4,512,256]{2,1,0:T(8,128)(2,1)S(1)}, u32[]{:S(2)}, u32[]{:S(2)}) %all-to-all-start.2) | async-done | bytes 1048608 | tf_op jit(solution)/shard_map/all_to_all | solution.py:256
  480.8 1.8 convert_multiply_fusion
  482.6 1.9 copy.76
  484.5 2.4 bitcast_reduce_fusion
  486.9 67.9 %attend_back.1 = (bf16[2048,256]{1,0:T(8,128)(2,1)}, bf16[2048,512]{1,0:T(8,128)(2,1)}) custom-call(s32[8]{0:T(128)} %get-tuple-element.74.first_ref, s32[8]{0:T(128)} %get-tuple-element.73.last_ref, bf16[2048,256]{1,0:T(8,128)(2,1)} %slice.36.q_ref, bf16[2048,512]{1,0:T(8,128)(2,1)} %slice.37.kv_ref, bf16[2048,256]{1,0:T(8,128)(2,1)} %bitcast.61, ...), custom_call_target="tpu_custom_call" | custom-call | tf_op jit(solution)/shard_map/attend_back/pallas_call | solution.py:218
  554.9 2.2 pad_maximum_fusion
  557.0 2.9 copy.79
  559.9 3.7 all-to-all-start.3
  564.4 67.0 %all-to-all-done.3 = bf16[4,512,768]{1,2,0:T(8,128)(2,1)S(1)} async-done(((bf16[4,512,768]{1,2,0:T(8,128)(2,1)}), bf16[4,512,768]{1,2,0:T(8,128)(2,1)S(1)}, u32[]{:S(2)}, u32[]{:S(2)}) %all-to-all-start.3) | async-done | bytes 3145760 | tf_op jit(solution)/shard_map/all_to_all | solution.py:263
  633.3 6.0 convolution_convert_fusion.2
  641.4 3.2 convert_reduce_fusion
  645.0 10.6 %add_convert_fusion.3 = bf16[512,1024]{1,0:T(8,128)(2,1)} fusion(f32[512,1024]{1,0:T(8,128)} %copy-done.3, bf16[512,4096]{1,0:T(8,128)(2,1)} %multiply_convert_fusion, bf16[4096,1024]{1,0:T(8,128)(2,1)} %all-gather.12.cloned.1.call-done, f32[1024]{0:T(1024)S(1)} %convert_element_type.124), kind=kOutput, calls=%fused_computation.49 | convolution fusion | flops 4296540160 | bytes 15732736 | tf_op jit(solution)/shard_map/dot_general | solution.py:342
  655.6 11.0 %reduce-scatter.15.cloned.1.call-done = bf16[32,1024]{1,0:T(8,128)(2,1)} async-done(((bf16[128,1024]{1,0:T(8,128)(2,1)}), bf16[32,1024]{1,0:T(8,128)(2,1)}) %reduce-scatter.15.cloned.1.call-update) | async-done | bytes 65552 | tf_op jit(solution)/shard_map/reduce_scatter | solution.py:270
  668.1 8.9 %fusion.25 = (f32[1024]{0:T(1024)S(1)}, f32[512]{0:T(512)S(1)}, f32[512,1024]{1,0:T(8,128)}) fusion(f32[1024]{0:T(1024)S(1)} %copy-done.18, f32[512]{0:T(512)S(1)} %copy-done.20, bf16[512,1024]{1,0:T(8,128)(2,1)} %param.16, bf16[512,3072]{0,1:T(8,128)(2,1)} %bitcast.66, bf16[1024,3072]{1,0:T(8,128)(2,1)} %all-gather.6.cloned.1.call-done), kind=kOutput, calls=%fused_computation.81 | convolution fusion | flops 3224369664 | bytes 12595200 | tf_op jit(solution)/shard_map/dot_general | solution.py:35
  677.0 52.9 %reduce-scatter.9.cloned.1.call-done = bf16[128,3072]{1,0:T(8,128)(2,1)} async-done(((bf16[1024,3072]{1,0:T(8,128)(2,1)}), bf16[128,3072]{1,0:T(8,128)(2,1)}) %reduce-scatter.9.cloned.1.call-update) | async-done | bytes 786448 | tf_op jit(solution)/shard_map/reduce_scatter | solution.py:269
  730.0 3.0 fusion.14
  733.7 2.0 convert_reduce_fusion.3
  735.7 41.3 %all-reduce.17 = (f32[1024]{0:T(1024)S(1)}, f32[1024]{0:T(1024)S(1)}, f32[1024]{0:T(1024)S(1)}, f32[1024]{0:T(1024)S(1)}, f32[1024]{0:T(1024)S(1)}, /*index=5*/f...) all-reduce(f32[1024]{0:T(1024)S(1)} %get-tuple-element.35, ...), channel_id=2, replica_groups=mesh['grp'=8,'seq'=4] {'grp','seq'}, use_global_device_ids=true, to_apply=%region_12.13.clone | all-reduce | flops 12288 | bytes 98304
  782.3 1.8 convert_element_type.143
  784.1 3.9 reduce-scatter.19.cloned.1.call-done
  787.9 1.8 convert_element_type.141
  789.7 22.5 %reduce-scatter.11.cloned.1.call-done = bf16[32,3072]{1,0:T(8,128)(2,1)} async-done(((bf16[128,3072]{1,0:T(8,128)(2,1)}), bf16[32,3072]{1,0:T(8,128)(2,1)}) %reduce-scatter.11.cloned.1.call-update) | async-done | bytes 196624 | tf_op jit(solution)/shard_map/reduce_scatter | solution.py:270
  812.2 1.7 convert_element_type.137
  (151 shorter events, 36.3 us)
Async XLA Ops:
  7.2 76.1 %all-gather.6.cloned.1.call-start = ((), (), s32[]{:S(2)}) async-start(), calls=%async_computation.12 | async-start | bytes 6488064 | tf_op jit(solution)/shard_map/all_gather | solution.py:297
  7.9 355.2 %all-gather.8.cloned.1.call-start = ((), (), s32[]{:S(2)}) async-start(), calls=%async_computation.13 | async-start | bytes 2162688 | tf_op jit(solution)/shard_map/all_gather | solution.py:300
  8.7 359.1 %all-gather.10.cloned.1.call-start = ((), (), s32[]{:S(2)}) async-start(), calls=%async_computation.14 | async-start | bytes 8650752 | tf_op jit(solution)/shard_map/all_gather | solution.py:304
  9.4 369.1 %all-gather.12.cloned.1.call-start = ((), (), s32[]{:S(2)}) async-start(), calls=%async_computation.15 | async-start | bytes 8650752 | tf_op jit(solution)/shard_map/all_gather | solution.py:306
  59.1 24.2 %copy-start.17 = (f32[1024]{0:T(1024)}, f32[1024]{0:T(1024)S(1)}, u32[]{:S(2)}) copy-start(f32[1024]{0:T(1024)S(1)} %convert_element_type.112) | copy-start | bytes 12292
  59.1 24.2 %copy-start.25 = (f32[1024]{0:T(1024)}, f32[1024]{0:T(1024)S(1)}, u32[]{:S(2)}) copy-start(f32[1024]{0:T(1024)S(1)} %convert_element_type.113) | copy-start | bytes 12292
  60.6 22.7 %copy-start.19 = (f32[512]{0:T(512)}, f32[512]{0:T(512)S(1)}, u32[]{:S(2)}) copy-start(f32[512]{0:T(512)S(1)} %broadcast_multiply_fusion.1) | copy-start | bytes 6148
  62.3 0.6 copy-start.21
  62.9 20.4 %copy-start.23 = (f32[512]{0:T(512)}, f32[512]{0:T(512)S(1)}, u32[]{:S(2)}) copy-start(f32[512]{0:T(512)S(1)} %fusion.19) | copy-start | bytes 6148
  101.6 3.8 copy-start.16
  101.6 83.7 %all-to-all-start = ((bf16[4,512,768]{1,2,0:T(8,128)(2,1)}), bf16[4,512,768]{1,2,0:T(8,128)(2,1)S(1)}, u32[]{:S(2)}, u32[]{:S(2)}) async-start(bf16[4,512,768]{1,2,0:T(8,128)(2,1)} %bitcast.57), calls=%async_computation | async-start | bytes 6291456 | tf_op jit(solution)/shard_map/all_to_all | solution.py:256
  260.4 6.0 copy-start.28
  260.4 103.7 %copy-start = (bf16[512,1024]{1,0:T(8,128)(2,1)S(1)}, bf16[512,1024]{1,0:T(8,128)(2,1)}, u32[]{:S(2)}) copy-start(bf16[512,1024]{1,0:T(8,128)(2,1)} %param.16) | copy-start | bytes 3145732
  262.8 100.3 %all-to-all-start.1 = ((bf16[4,512,256]{1,2,0:T(8,128)(2,1)}), bf16[4,512,256]{1,2,0:T(8,128)(2,1)S(1)}, u32[]{:S(2)}, u32[]{:S(2)}) async-start(bf16[4,512,256]{1,2,0:T(8,128)(2,1)} %copy.72), calls=%async_computation.1 | async-start | bytes 2097152 | tf_op jit(solution)/shard_map/all_to_all | solution.py:263
  266.4 297.3 %reduce-scatter.13.cloned.1.call-start = ((), (), s32[]{:S(2)}) async-start(), calls=%async_computation.18 | async-start | bytes 2359296 | tf_op jit(solution)/shard_map/reduce_scatter | solution.py:269
  363.1 1.0 copy-start.9
  367.4 75.3 %copy-start.3 = (f32[512,1024]{1,0:T(8,128)}, f32[512,1024]{1,0:T(8,128)S(1)}, u32[]{:S(2)}) copy-start(f32[512,1024]{1,0:T(8,128)S(1)} %get-tuple-element.70) | copy-start | bytes 6291460
  367.8 10.7 %copy-start.11 = (bf16[512,1024]{1,0:T(8,128)(2,1)S(1)}, bf16[512,1024]{1,0:T(8,128)(2,1)}, u32[]{:S(2)}) copy-start(bf16[512,1024]{1,0:T(8,128)(2,1)} %param.17) | copy-start | bytes 3145732
  443.4 1.3 copy-start.4
  443.4 2.0 copy-start.10
  445.4 4.0 copy-start.8
  448.1 191.3 %reduce-scatter.21.cloned.1.call-start = ((), (), s32[]{:S(2)}) async-start(), calls=%async_computation.22 | async-start | bytes 9437184 | tf_op jit(solution)/shard_map/reduce_scatter | solution.py:269
  448.7 1.6 copy-start.14
  448.7 195.9 %reduce-scatter.17.cloned.1.call-start = ((), (), s32[]{:S(2)}) async-start(), calls=%async_computation.20 | async-start | bytes 9437184 | tf_op jit(solution)/shard_map/reduce_scatter | solution.py:269
  452.5 6.8 copy-start.15
  455.6 25.2 %all-to-all-start.2 = ((bf16[4,512,256]{2,1,0:T(8,128)(2,1)}), bf16[4,512,256]{2,1,0:T(8,128)(2,1)S(1)}, u32[]{:S(2)}, u32[]{:S(2)}) async-start(bf16[4,512,256]{2,1,0:T(8,128)(2,1)} %bitcast.54), calls=%async_computation.2 | async-start | bytes 2097152 | tf_op jit(solution)/shard_map/all_to_all | solution.py:256
  480.8 3.7 copy-start.6
  559.9 71.5 %all-to-all-start.3 = ((bf16[4,512,768]{1,2,0:T(8,128)(2,1)}), bf16[4,512,768]{1,2,0:T(8,128)(2,1)S(1)}, u32[]{:S(2)}, u32[]{:S(2)}) async-start(bf16[4,512,768]{1,2,0:T(8,128)(2,1)} %copy.79), calls=%async_computation.3 | async-start | bytes 6291456 | tf_op jit(solution)/shard_map/all_to_all | solution.py:263
  563.6 103.0 %reduce-scatter.15.cloned.1.call-start = ((), (), s32[]{:S(2)}) async-start(), calls=%async_computation.19 | async-start | bytes 327680 | tf_op jit(solution)/shard_map/reduce_scatter | solution.py:270
  564.4 165.6 %reduce-scatter.9.cloned.1.call-start = ((), (), s32[]{:S(2)}) async-start(), calls=%async_computation.16 | async-start | bytes 7077888 | tf_op jit(solution)/shard_map/reduce_scatter | solution.py:269
  631.4 1.9 copy-start.1
  631.4 1.9 copy-start.18
  631.4 1.9 copy-start.20
  631.4 1.9 copy-start.24
  631.4 1.9 copy-start.26
  631.6 1.6 copy-start.13
  639.3 0.7 copy-start.27
  639.3 143.0 %reduce-scatter.23.cloned.1.call-start = ((), (), s32[]{:S(2)}) async-start(), calls=%async_computation.23 | async-start | bytes 1310720 | tf_op jit(solution)/shard_map/reduce_scatter | solution.py:270
  639.9 148.0 %reduce-scatter.19.cloned.1.call-start = ((), (), s32[]{:S(2)}) async-start(), calls=%async_computation.21 | async-start | bytes 1310720 | tf_op jit(solution)/shard_map/reduce_scatter | solution.py:270
  644.7 167.5 %reduce-scatter.11.cloned.1.call-start = ((), (), s32[]{:S(2)}) async-start(), calls=%async_computation.17 | async-start | bytes 983040 | tf_op jit(solution)/shard_map/reduce_scatter | solution.py:270
  668.1 61.9 %copy-start.22 = (f32[512]{0:T(512)S(1)}, f32[512]{0:T(512)}, u32[]{:S(2)}) copy-start(f32[512]{0:T(512)} %copy-done.21) | copy-start | bytes 6148
  730.0 3.5 copy-start.2
  730.0 3.5 copy-start.5
  730.0 3.5 copy-start.7
  730.0 3.7 copy-start.12
Sparse Core Ops, SparseCore 0:
  10.9 72.3 all-gather.5
  86.2 84.5 all-gather.7
  173.7 78.5 all-gather.9
  255.1 88.6 all-gather.11
  448.2 46.4 reduce-scatter.12
  498.5 71.2 reduce-scatter.20
  573.2 71.2 reduce-scatter.16
  646.9 19.6 reduce-scatter.14
  670.0 59.9 reduce-scatter.8
  732.2 27.5 reduce-scatter.22
  762.1 25.7 reduce-scatter.18
  790.2 21.9 reduce-scatter.10

commit v2 on v1

v2 whole, which is shorter than its diff:
```python
from functools import partial
import math

import jax
import jax.numpy as jnp
from jax import lax
from jax.experimental import pallas as pl
from jax.experimental.pallas import tpu as pltpu
from jax.sharding import PartitionSpec as P

HEADS = 16


EPS = 1e-06
MASKED = -1e30


def layer_norm(value, gain, shift):
    center = value - jnp.mean(value, axis=-1, keepdims=True)
    spread = jnp.mean(center * center, axis=-1, keepdims=True)
    return center * lax.rsqrt(spread + EPS) * gain + shift


def scaled_norm(value, gain):
    return layer_norm(value, gain, 0.0)


def rows_dot(left, right):
    return lax.dot_general(
        left, right, (((0,), (0,)), ((), ())), preferred_element_type=jnp.float32
    )


def dot_back(left, right):
    return lax.dot_general(
        left, right, (((1,), (1,)), ((), ())), preferred_element_type=jnp.float32
    )


BLOCK = 256


def head_lanes(shape, head, size):
    lane = lax.broadcasted_iota(jnp.int32, shape, len(shape) - 1)
    return lane // size == head


def only_head(value, head, size):
    return jnp.where(head_lanes(value.shape, head, size), value, jnp.zeros_like(value))


def forward_kernel(
    heads, first_ref, last_ref, q_ref, kv_ref, row_ref, col_ref, out_ref, lse_ref,
    s_ref, own_ref, peak_ref, total_ref, sum_ref
):
    step = pl.program_id(0)
    first = first_ref[step]
    last = last_ref[step]
    width = q_ref.shape[1]
    size = width // heads
    half = BLOCK // 2
    query = q_ref[...] * (1.0 / math.sqrt(size))
    for head in range(heads):
        own_ref[head] = only_head(query, head, size)
    peak_ref[...] = jnp.full_like(peak_ref, MASKED)
    total_ref[...] = jnp.zeros_like(total_ref)
    sum_ref[...] = jnp.zeros_like(sum_ref)
    mine = row_ref[...]

    def scores_at(at, carry):
        rows = pl.ds(pl.multiple_of(at * BLOCK, BLOCK), BLOCK)
        keys = kv_ref[rows, :width]
        same = mine == col_ref[at]
        for head in range(heads):
            scores = dot_back(own_ref[head], keys)
            scores = jnp.where(same, scores, MASKED)
            s_ref[head, at] = scores
            most = jnp.maximum(scores[:, :half], scores[:, half:])
            peak_ref[head] = jnp.maximum(peak_ref[head], most)
        return carry

    lax.fori_loop(first, last, scores_at, 0)
    peaks = [jnp.max(peak_ref[head], axis=-1, keepdims=True) for head in range(heads)]

    def sum_at(at, carry):
        rows = pl.ds(pl.multiple_of(at * BLOCK, BLOCK), BLOCK)
        values = kv_ref[rows, width:]
        result = sum_ref[...]
        for head in range(heads):
            expo = jnp.exp(s_ref[head, at] - peaks[head])
            total_ref[head] += expo[:, :half] + expo[:, half:]
            result = result + jnp.dot(
                expo.astype(jnp.bfloat16),
                only_head(values, head, size),
                preferred_element_type=jnp.float32,
            )
        sum_ref[...] = result
        return carry

    lax.fori_loop(first, last, sum_at, 0)
    merged = jnp.zeros((BLOCK, width), jnp.float32)
    for head in range(heads):
        total = jnp.sum(total_ref[head], axis=-1, keepdims=True)
        lse_ref[:, head : head + 1] = peaks[head] + jnp.log(total)
        merged = jnp.where(head_lanes(merged.shape, head, size), sum_ref[...] / total, merged)
    out_ref[...] = merged.astype(out_ref.dtype)


def backward_kernel(
    heads, first_ref, last_ref, q_ref, kv_ref, g_ref, lse_ref, delta_ref, row_ref, col_ref,
    dq_ref, dkv_ref, sum_ref, own_ref, key_sum_ref, value_sum_ref
):
    step = pl.program_id(0)
    first = first_ref[step]
    last = last_ref[step]
    width = q_ref.shape[1]
    size = width // heads
    scale = 1.0 / math.sqrt(size)

    @pl.when(step == 0)
    def clear():
        sum_ref[...] = jnp.zeros_like(sum_ref)

    scaled = kv_ref[:, :width] * scale
    for head in range(heads):
        own_ref[head] = only_head(scaled, head, size)
    key_sum_ref[...] = jnp.zeros_like(key_sum_ref)
    value_sum_ref[...] = jnp.zeros_like(value_sum_ref)
    mine = row_ref[...]

    def at_queries(at, carry):
        rows = pl.ds(pl.multiple_of(at * BLOCK, BLOCK), BLOCK)
        query = q_ref[rows, :]
        grad = g_ref[rows, :]
        values = kv_ref[:, width:]
        same = mine == col_ref[at]
        sum_keys = key_sum_ref[...]
        sum_values = value_sum_ref[...]
        sum_queries = sum_ref[rows, :]
        for head in range(heads):
            own_keys = own_ref[head]
            own_grad = only_head(grad, head, size)
            scores = jnp.where(same, dot_back(own_keys, query), MASKED)
            weights = jnp.exp(scores - lse_ref[at, head : head + 1, :])
            grad_probs = dot_back(values, own_grad)
            grad_scores = (weights * (grad_probs - delta_ref[at, head : head + 1, :])).astype(
                jnp.bfloat16
            )
            sum_values = sum_values + jnp.dot(
                weights.astype(jnp.bfloat16), own_grad, preferred_element_type=jnp.float32
            )
            sum_keys = sum_keys + jnp.dot(
                grad_scores, only_head(query, head, size), preferred_element_type=jnp.float32
            )
            sum_queries = sum_queries + rows_dot(grad_scores, own_keys)
        key_sum_ref[...] = sum_keys
        value_sum_ref[...] = sum_values
        sum_ref[rows, :] = sum_queries
        return carry

    lax.fori_loop(first, last, at_queries, 0)
    dkv_ref[:, :width] = (key_sum_ref[...] * scale).astype(jnp.bfloat16)
    dkv_ref[:, width:] = value_sum_ref[...].astype(jnp.bfloat16)

    @pl.when(step == pl.num_programs(0) - 1)
    def store():
        dq_ref[...] = sum_ref[...].astype(jnp.bfloat16)


def whole(shape):
    return pl.BlockSpec(shape, lambda step, first, last: (0,) * len(shape))


def by_rows(width):
    return pl.BlockSpec((BLOCK, width), lambda step, first, last: (step, 0))


def block_bounds(labels):
    per_block = labels.reshape(-1, BLOCK)
    least, most = per_block[:, 0], per_block[:, -1]
    first = jnp.sum(labels[None, :] < least[:, None], axis=1) // BLOCK
    last = (jnp.sum(labels[None, :] <= most[:, None], axis=1) + BLOCK - 1) // BLOCK
    return first.astype(jnp.int32), last.astype(jnp.int32)


def attend(joint, labels, bounds, heads):
    count, width = joint.shape[0], joint.shape[1] // 3
    blocks = count // BLOCK
    return pl.pallas_call(
        partial(forward_kernel, heads),
        grid_spec=pltpu.PrefetchScalarGridSpec(
            num_scalar_prefetch=2,
            grid=(blocks,),
            in_specs=[
                by_rows(width),
                whole((count, 2 * width)),
                by_rows(1),
                whole((blocks, 1, BLOCK)),
            ],
            out_specs=[by_rows(width), by_rows(heads)],
            scratch_shapes=[
                pltpu.VMEM((heads, blocks, BLOCK, BLOCK), jnp.float32),
                pltpu.VMEM((heads, BLOCK, width), jnp.bfloat16),
                pltpu.VMEM((heads, BLOCK, BLOCK // 2), jnp.float32),
                pltpu.VMEM((heads, BLOCK, BLOCK // 2), jnp.float32),
                pltpu.VMEM((BLOCK, width), jnp.float32),
            ],
        ),
        out_shape=[
            jax.ShapeDtypeStruct((count, width), jnp.bfloat16),
            jax.ShapeDtypeStruct((count, heads), jnp.float32),
        ],
        name="attend",
    )(
        *bounds,
        joint[:, :width],
        joint[:, width:],
        labels.reshape(count, 1),
        labels.reshape(blocks, 1, BLOCK),
    )


def attend_back(joint, grad, spread, inner, labels, bounds, heads):
    count, width = joint.shape[0], joint.shape[1] // 3
    blocks = count // BLOCK

    def in_rows(value):
        return value.reshape(blocks, BLOCK, heads).transpose(0, 2, 1)

    return pl.pallas_call(
        partial(backward_kernel, heads),
        grid_spec=pltpu.PrefetchScalarGridSpec(
            num_scalar_prefetch=2,
            grid=(blocks,),
            in_specs=[
                whole((count, width)),
                by_rows(2 * width),
                whole((count, width)),
                whole((blocks, heads, BLOCK)),
                whole((blocks, heads, BLOCK)),
                by_rows(1),
                whole((blocks, 1, BLOCK)),
            ],
            out_specs=[whole((count, width)), by_rows(2 * width)],
            scratch_shapes=[
                pltpu.VMEM((count, width), jnp.float32),
                pltpu.VMEM((heads, BLOCK, width), jnp.bfloat16),
                pltpu.VMEM((BLOCK, width), jnp.float32),
                pltpu.VMEM((BLOCK, width), jnp.float32),
            ],
        ),
        out_shape=[
            jax.ShapeDtypeStruct((count, width), jnp.bfloat16),
            jax.ShapeDtypeStruct((count, 2 * width), jnp.bfloat16),
        ],
        name="attend_back",
    )(
        *bounds,
        joint[:, :width],
        joint[:, width:],
        grad,
        in_rows(spread),
        in_rows(inner),
        labels.reshape(count, 1),
        labels.reshape(blocks, 1, BLOCK),
    )


def to_heads(rows, parts, seq):
    count, width = rows.shape
    share = width // parts // seq
    split = rows.reshape(count, parts, seq, share).transpose(2, 0, 1, 3)
    moved = lax.all_to_all(split.reshape(seq, count, parts * share), "seq", 0, 0)
    return moved.reshape(seq * count, parts * share)


def to_rows(rows, parts, seq):
    count, width = rows.shape
    share = width // parts
    moved = lax.all_to_all(rows.reshape(seq, count // seq, width), "seq", 0, 0)
    split = moved.reshape(seq, count // seq, parts, share).transpose(1, 2, 0, 3)
    return split.reshape(count // seq, parts * seq * share)


def scatter_sum(value):
    near = lax.psum_scatter(value.astype(jnp.bfloat16), "grp", scatter_dimension=0, tiled=True)
    return lax.psum_scatter(near, "seq", scatter_dimension=0, tiled=True).astype(jnp.float32)


def with_vectors(value, vectors):
    count = value.shape[0]
    columns = jnp.concatenate([vector.reshape(count, -1) for vector in vectors], axis=1)
    columns = jnp.pad(columns, ((0, 0), (0, 128 - columns.shape[1])))
    return jnp.concatenate([value.astype(jnp.bfloat16), columns.astype(jnp.bfloat16)], axis=1)


def split_vectors(value, width, counts):
    vectors, at = [], width
    for count in counts:
        vectors.append(value[:, at : at + count].reshape(-1))
        at += count
    return value[:, :width], vectors


def per_device(
    tokens,
    cotangent,
    image_of_token,
    ln1_gain,
    ln1_bias,
    qkv_weight,
    q_bias,
    v_bias,
    out_weight,
    out_bias,
    ln2_gain,
    ln2_bias,
    up_weight,
    up_bias,
    down_weight,
    down_bias,
):
    f32 = jnp.float32
    bf16 = jnp.bfloat16
    width = tokens.shape[1]
    everyone = ("grp", "seq")
    ratio = down_weight.shape[0] // up_weight.shape[0]
    first_pack = with_vectors(
        qkv_weight,
        (ln1_gain, ln1_bias, q_bias, v_bias, out_bias, ln2_gain, ln2_bias, down_bias, up_bias),
    )
    first_pack = lax.all_gather(first_pack, everyone, axis=0, tiled=True)
    w_joint, vectors = split_vectors(first_pack, 3 * width, (1,) * 8 + (ratio,))
    (
        gain_first,
        shift_first,
        bias_query,
        bias_value,
        bias_out,
        gain_second,
        shift_second,
        bias_down,
        bias_up,
    ) = vectors
    rows = up_weight.shape[0]
    second_pack = jnp.concatenate(
        [up_weight, out_weight]
        + [down_weight[part * rows : (part + 1) * rows] for part in range(ratio)],
        axis=1,
    )
    second_pack = lax.all_gather(second_pack, everyone, axis=0, tiled=True)
    w_up = second_pack[:, : ratio * width]
    w_out = second_pack[:, ratio * width : (ratio + 1) * width]
    w_down = second_pack[:, (ratio + 1) * width :].reshape(-1, rows, ratio, width)
    w_down = w_down.transpose(0, 2, 1, 3).reshape(ratio * width, width)
    inputs = tokens.astype(f32)
    normed_first = layer_norm(inputs, gain_first.astype(f32), shift_first.astype(f32)).astype(bf16)
    zeros = jnp.zeros((width,), f32)
    joint_bias = jnp.concatenate([bias_query.astype(f32), zeros, bias_value.astype(f32)])
    joint = (jnp.dot(normed_first, w_joint, preferred_element_type=f32) + joint_bias).astype(bf16)
    seq = lax.axis_size("seq")
    heads = HEADS // seq
    bounds = block_bounds(image_of_token)
    own_joint = to_heads(joint, 3, seq)
    own_attended, spread = attend(own_joint, image_of_token, bounds, heads)
    attended = to_rows(own_attended, 1, seq)
    resid = inputs + jnp.dot(attended, w_out, preferred_element_type=f32) + bias_out.astype(f32)
    normed_second = layer_norm(resid, gain_second.astype(f32), shift_second.astype(f32)).astype(
        bf16
    )
    hidden = jnp.dot(normed_second, w_up, preferred_element_type=f32) + bias_up.astype(f32)
    below = 0.5 * (1.0 + lax.erf(hidden * math.sqrt(0.5)))
    slope = below + hidden * (jnp.exp(-0.5 * hidden * hidden) * (1.0 / math.sqrt(2.0 * math.pi)))
    active, slope = lax.optimization_barrier(((hidden * below).astype(bf16), slope))
    down_grad = rows_dot(active, cotangent).astype(bf16)
    active, down_grad = lax.optimization_barrier((active, down_grad))
    down_grad = scatter_sum(down_grad)
    grad_hidden = (dot_back(cotangent, w_down) * slope).astype(bf16)
    up_grad = rows_dot(normed_second, grad_hidden).astype(bf16)
    grad_hidden, up_grad = lax.optimization_barrier((grad_hidden, up_grad))
    up_grad = scatter_sum(up_grad)
    output = (
        resid + jnp.dot(active, w_down, preferred_element_type=f32) + bias_down.astype(f32)
    ).astype(bf16)
    down_bias_grad = jnp.sum(cotangent.astype(f32), axis=0)
    up_bias_grad = jnp.sum(grad_hidden.astype(f32), axis=0)
    grad_normed = dot_back(grad_hidden, w_up)
    _, second_back = jax.vjp(scaled_norm, resid, gain_second.astype(f32))
    grad_through, gain_second_grad = second_back(grad_normed)
    shift_second_grad = jnp.sum(grad_normed, axis=0)
    grad_resid = cotangent.astype(f32) + grad_through
    grad_branch = grad_resid.astype(bf16)
    out_bias_grad = jnp.sum(grad_branch.astype(f32), axis=0)
    out_grad = with_vectors(
        rows_dot(attended, grad_branch),
        (out_bias_grad, gain_second_grad, shift_second_grad, down_bias_grad, up_bias_grad),
    )
    grad_branch, out_grad = lax.optimization_barrier((grad_branch, out_grad))
    out_grad, early = split_vectors(scatter_sum(out_grad), width, (1, 1, 1, 1, bias_up.shape[0] // width))
    out_bias_grad, gain_second_grad, shift_second_grad, down_bias_grad, up_bias_grad = early
    grad_attended = dot_back(grad_branch, w_out).astype(bf16)
    own_grad = to_heads(grad_attended, 1, seq)
    inner = jnp.sum(
        (own_grad.astype(f32) * own_attended.astype(f32)).reshape(own_grad.shape[0], heads, -1),
        axis=-1,
    )
    grad_q, grad_kv = attend_back(
        own_joint, own_grad, spread, inner, image_of_token, bounds, heads
    )
    grad_joint = to_rows(jnp.concatenate([grad_q, grad_kv], axis=1), 3, seq)
    column_sums = jnp.sum(grad_joint.astype(f32), axis=0)
    query_bias_grad = column_sums[:width]
    value_bias_grad = column_sums[2 * width :]
    grad_first = dot_back(grad_joint, w_joint)
    _, first_back = jax.vjp(scaled_norm, inputs, gain_first.astype(f32))
    grad_entry, gain_first_grad = first_back(grad_first)
    shift_first_grad = jnp.sum(grad_first, axis=0)
    input_grad = (grad_resid + grad_entry).astype(bf16)
    joint_grad = with_vectors(
        rows_dot(normed_first, grad_joint),
        (gain_first_grad, shift_first_grad, query_bias_grad, value_bias_grad),
    )
    joint_grad, late = split_vectors(scatter_sum(joint_grad), 3 * width, (1, 1, 1, 1))
    gain_first_grad, shift_first_grad, query_bias_grad, value_bias_grad = late
    return (
        output,
        input_grad,
        gain_first_grad,
        shift_first_grad,
        joint_grad,
        query_bias_grad,
        value_bias_grad,
        out_grad,
        out_bias_grad,
        gain_second_grad,
        shift_second_grad,
        up_grad,
        up_bias_grad,
        down_grad,
        down_bias_grad,
    )


def solution(mesh):
    placed = (
        P(("grp", "seq"), None),
        P(("grp", "seq"), None),
        P("grp"),
        P(("grp", "seq")),
        P(("grp", "seq")),
        P(("grp", "seq"), None),
        P(("grp", "seq")),
        P(("grp", "seq")),
        P(("grp", "seq"), None),
        P(("grp", "seq")),
        P(("grp", "seq")),
        P(("grp", "seq")),
        P(("grp", "seq"), None),
        P(("grp", "seq")),
        P(("grp", "seq"), None),
        P(("grp", "seq")),
    )
    return jax.shard_map(
        per_device,
        mesh=mesh,
        in_specs=placed,
        out_specs=(
            P(("grp", "seq"), None),
            P(("grp", "seq"), None),
            P(("grp", "seq")),
            P(("grp", "seq")),
            P(("grp", "seq"), None),
            P(("grp", "seq")),
            P(("grp", "seq")),
            P(("grp", "seq"), None),
            P(("grp", "seq")),
            P(("grp", "seq")),
            P(("grp", "seq")),
            P(("grp", "seq"), None),
            P(("grp", "seq")),
            P(("grp", "seq"), None),
            P(("grp", "seq")),
        ),
        check_vma=False,
    )
```

time: 827 us -> 783 us (0.947)
  blocking collectives: 180 us -> 67.8 us
  waiting for transfers between devices: 281 us -> 387 us
  Pallas kernels: 135 us -> 70.5 us
  local copies, waits for them, and re-layouts: 48.8 us -> 100 us
  matrix products: 107 us -> 83.8 us
    all_gather x1 -> x0, blocking collectives: 96.6 us -> none  [per_device(): lax.all_gather(up_bias, ('grp', 'seq'), axis=0, tiled=True)]
    unnamed x2 -> x0, blocking collectives: 83.7 us -> none
    all_to_all x0 -> x1, blocking collectives: none -> 67.8 us  [to_rows(): moved = lax.all_to_all(rows.reshape(seq, count // seq, width), 'seq', 0, 0)]
    all_to_all x2, waiting for transfers between devices: 98.1 us -> 147 us  [to_heads(): lax.all_to_all(split.reshape(seq, count, parts * share), 'seq', 0, 0)]
    all_gather x4 -> x2, waiting for transfers between devices: 20.5 us -> 66.9 us  [the longest x1 66.9 us: per_device(): first_pack = lax.all_gather(first_pack, everyone, axis=0, tiled=True)]
    all_to_all x2 -> x1, waiting for transfers between devices: 67 us -> 21.8 us  [to_rows(): moved = lax.all_to_all(rows.reshape(seq, count // seq, width), 'seq', 0, 0)]
    pallas_call x1, Pallas kernels: 66.9 us -> 26.5 us  [attend(): pl.pallas_call(partial(forward_kernel, heads), grid_spec=pltpu.PrefetchSc...]
    reduce_scatter x4 -> x3, waiting for transfers between devices: 37.4 us -> 66.9 us  [scatter_sum(): lax.psum_scatter(near, 'seq', scatter_dimension=0, tiled=True)]
  transfers between devices with their start and end apart: 16 -> 13, of which waited for: 8 -> 10; matrix products, arithmetic and copies ran while one was open for 14% -> 15% of each run, Pallas kernels for 16% -> 9%
where the time goes in v2:
time: 783 us; the launch traced here: 773 us
  waiting for transfers between devices  387 us (49%)
  local copies, waits for them, and re-layouts  100 us (13%)
  matrix products  83.8 us (11%)
  Pallas kernels  70.5 us (9%)
  blocking collectives  67.8 us (9%)
  other arithmetic  35.5 us (5%)
  between operations  14.9 us (2%)
  starting transfers between devices  13.1 us (2%)
    all_to_all x2, waiting for transfers between devices, to_heads(): lax.all_to_all(split.reshape(seq, count, parts * share), 'seq', 0, 0)  147 us
    reduce_scatter x3, waiting for transfers between devices, scatter_sum(): lax.psum_scatter(value.astype(jnp.bfloat16), 'grp', scatter_dimension=0,...  70.6 us
    all_to_all x1, blocking collectives, to_rows(): moved = lax.all_to_all(rows.reshape(seq, count // seq, width), 'seq', 0, 0)  67.8 us
    all_gather x1, waiting for transfers between devices, per_device(): first_pack = lax.all_gather(first_pack, everyone, axis=0, tiled=True)  66.9 us
    reduce_scatter x3, waiting for transfers between devices, scatter_sum(): lax.psum_scatter(near, 'seq', scatter_dimension=0, tiled=True)  66.9 us
    pallas_call x1, Pallas kernels, attend_back(): pl.pallas_call(partial(backward_kernel, heads), grid_spec=pltpu.PrefetchS...  43.9 us
    pallas_call x1, Pallas kernels, attend(): pl.pallas_call(partial(forward_kernel, heads), grid_spec=pltpu.PrefetchSc...  26.5 us
    dot_general x4, matrix products, rows_dot(): lax.dot_general(left, right, (((0,), (0,)), ((), ())), preferred_element_...  25.2 us
  transfers between devices with their start and end apart: 13, of which 10 were waited for; matrix products, arithmetic and copies ran while one was open for 15% of the time, Pallas kernels for 9%

profile of v2, /device:TPU:0, one launch (start us, length us, event | category | flops | bytes accessed | tf_op | source)
XLA Modules:
  0.0 773.1 jit_solution(14953484518930881923)
XLA Ops:
  22.6 66.9 %all-gather.3.cloned.1.call-done = bf16[1024,3200]{1,0:T(8,128)(2,1)} async-done(((bf16[32,3200]{1,0:T(8,128)(2,1)}), bf16[1024,3200]{1,0:T(8,128)(2,1)}) %all-gather.3.cloned.1.call-update) | async-done | bytes 6553616 | tf_op jit(solution)/shard_map/all_gather | solution.py:332
  89.5 3.5 convert_reduce_fusion.1
  93.0 7.8 %add_convert_fusion = bf16[512,3072]{1,0:T(8,128)(2,1)} fusion(bf16[1024,3200]{1,0:T(8,128)(2,1)} %all-gather.3.cloned.1.call-done, f32[3072]{0:T(1024)S(1)} %pad_maximum_fusion.1, bf16[512,1024]{1,0:T(8,128)(2,1)S(1)} %copy-done.2, f32[1024]{0:T(1024)S(1)} %get-tuple-element.120, f32[1024]{0:T(1024)S(1)} %get-tuple-element.121, f32[512]{0:T(512)S(1)} %fusion.43, ...), kind=kOutput, calls=%fused_computation.18 | convolution fusion | flops 3227516928 | bytes 10510336 | tf_op jit(solution)/shard_map/dot_general | solution.py:360
  100.8 6.7 reshape.317
  107.5 5.9 copy.135
  113.4 4.8 all-to-all-start
  120.6 122.1 %all-to-all-done = bf16[4,512,768]{1,2,0:T(8,128)(2,1)} async-done(((bf16[4,512,768]{1,2,0:T(8,128)(2,1)}), bf16[4,512,768]{1,2,0:T(8,128)(2,1)}, u32[]{:S(2)}, u32[]{:S(2)}) %all-to-all-start) | async-done | bytes 3145760 | tf_op jit(solution)/shard_map/all_to_all | solution.py:273
  242.7 4.7 copy.136
  247.4 2.3 slice.149.q_ref
  249.7 3.0 slice.150.kv_ref
  252.8 26.5 %attend.1 = (bf16[2048,256]{1,0:T(8,128)(2,1)}, f32[2048,4]{1,0:T(8,128)}) custom-call(s32[8]{0:T(128)} %get-tuple-element.155.first_ref, s32[8]{0:T(128)} %get-tuple-element.154.last_ref, bf16[2048,256]{1,0:T(8,128)(2,1)} %slice.149.q_ref, bf16[2048,512]{1,0:T(8,128)(2,1)} %slice.150.kv_ref, s32[2048,1]{1,0:T(8,128)} %copy.137.row_ref, s32[8,1,256]{2,1,0:T(1,128)} %bitcast.87), custom_call_target="tpu_custom_call" | custom-call | tf_op jit(solution)/shard_map/attend/pallas_call | solution.py:189
  279.3 2.3 copy.138
  281.6 3.5 all-to-all-start.1
  286.5 21.8 %all-to-all-done.1 = bf16[4,512,256]{1,2,0:T(8,128)(2,1)S(1)} async-done(((bf16[4,512,256]{1,2,0:T(8,128)(2,1)}), bf16[4,512,256]{1,2,0:T(8,128)(2,1)S(1)}, u32[]{:S(2)}, u32[]{:S(2)}) %all-to-all-start.1) | async-done | bytes 1048608 | tf_op jit(solution)/shard_map/all_to_all | solution.py:280
  309.3 3.3 fusion.52
  313.0 8.2 %slice.157 = bf16[1024,4096]{1,0:T(8,128)(2,1)} slice(bf16[1024,9216]{1,0:T(8,128)(2,1)} %all-gather.5.cloned.1.call-done), slice={[0:1024], [5120:9216]} | slice | bytes 16777216 | tf_op jit(solution)/shard_map/slice | solution.py:354
  321.2 15.0 %reshape.325 = bf16[32,32,4,1024]{3,2,1,0:T(4,128)(2,1)} reshape(bf16[1024,4096]{1,0:T(8,128)(2,1)} %slice.157) | data formatting | bytes 16777216 | tf_op jit(solution)/shard_map/reshape | solution.py:354
  336.2 10.4 %copy.139 = bf16[32,4,32,1024]{3,2,1,0:T(8,128)(2,1)} copy(bf16[32,4,32,1024]{3,1,2,0:T(4,128)(2,1)} %bitcast.71) | data formatting | bytes 16777216 | tf_op jit(solution)/shard_map/transpose | solution.py:355
  346.6 12.5 %fusion.4 = (f32[512,4096]{1,0:T(8,128)}, bf16[512,4096]{1,0:T(8,128)(2,1)}) fusion(f32[4096]{0:T(1024)S(1)} %reshape.361, bf16[1024,9216]{1,0:T(8,128)(2,1)} %all-gather.5.cloned.1.call-done, f32[512,1024]{1,0:T(8,128)S(1)} %get-tuple-element.150, f32[1024]{0:T(1024)S(1)} %get-tuple-element.115, f32[1024]{0:T(1024)S(1)} %get-tuple-element.116, ...), kind=kOutput, calls=%fused_computation.6 | convolution fusion | flops 4320657408 | bytes 23097344 | tf_op jit(solution)/shard_map/dot_general | solution.py:371
  359.1 7.0 fusion.5
  366.2 1.9 copy-done.10
  368.2 7.4 convolution_convert_fusion
  375.5 3.2 reduce.3
  378.7 8.7 %multiply_reduce_fusion = (bf16[1024]{0:T(1024)(128)(2,1)S(1)}, f32[512]{0:T(512)S(1)}, bf16[1024]{0:T(1024)(128)(2,1)S(1)}, f32[512,1024]{1,0:T(8,128)S(1)}) fusion(f32[512,1024]{1,0:T(8,128)S(1)} %get-tuple-element.150, f32[512]{0:T(512)S(1)} %fusion.44, f32[512]{0:T(512)S(1)} %broadcast_multiply_fusion, f32[1024]{0:T(1024)S(1)} %get-tuple-element.116, ...), kind=kOutput, calls=%fused_computation.48 | convolution fusion | flops 4299159040 | bytes 16791552 | tf_op jit(solution)/shard_map/dot_general | solution.py:35
  387.5 2.4 fusion.50
  392.2 2.6 convolution_convert_fusion.3
  396.7 2.5 copy.156
  399.9 9.1 %convolution_convert_fusion.1 = bf16[4096,1024]{1,0:T(8,128)(2,1)} fusion(bf16[512,4096]{1,0:T(8,128)(2,1)} %get-tuple-element.29, bf16[512,1024]{1,0:T(8,128)(2,1)S(1)} %copy-done.12), kind=kOutput, calls=%fused_computation.12 | convolution fusion | flops 4299161600 | bytes 13631488 | tf_op jit(solution)/shard_map/dot_general | solution.py:29
  410.2 3.0 fusion.35
  415.2 4.1 all-to-all-start.2
  420.3 25.1 %all-to-all-done.2 = bf16[4,512,256]{2,1,0:T(8,128)(2,1)S(1)} async-done(((bf16[4,512,256]{2,1,0:T(8,128)(2,1)}), bf16[4,512,256]{2,1,0:T(8,128)(2,1)S(1)}, u32[]{:S(2)}, u32[]{:S(2)}) %all-to-all-start.2) | async-done | bytes 1048608 | tf_op jit(solution)/shard_map/all_to_all | solution.py:273
  447.3 2.1 copy.145
  449.3 2.4 bitcast_reduce_fusion
  451.7 43.9 %attend_back.1 = (bf16[2048,256]{1,0:T(8,128)(2,1)}, bf16[2048,512]{1,0:T(8,128)(2,1)}) custom-call(s32[8]{0:T(128)} %get-tuple-element.155.first_ref, s32[8]{0:T(128)} %get-tuple-element.154.last_ref, bf16[2048,256]{1,0:T(8,128)(2,1)} %slice.149.q_ref, bf16[2048,512]{1,0:T(8,128)(2,1)} %slice.150.kv_ref, bf16[2048,256]{1,0:T(8,128)(2,1)} %bitcast.78, ...), custom_call_target="tpu_custom_call" | custom-call | tf_op jit(solution)/shard_map/attend_back/pallas_call | solution.py:230
  495.7 2.1 pad_maximum_fusion
  497.7 2.8 copy.148
  500.5 67.8 %all_to_all.20 = bf16[4,512,768]{1,2,0:T(8,128)(2,1)S(1)} all-to-all(bf16[4,512,768]{1,2,0:T(8,128)(2,1)} %copy.148), channel_id=1, replica_groups=mesh['grp'=8,'seq'=4] {'seq'}, dimensions={0} | all-to-all | bytes 6291456 | tf_op jit(solution)/shard_map/all_to_all | solution.py:280
  570.2 6.0 fusion.29
  578.2 6.2 convolution_convert_fusion.2
  584.4 3.1 fusion.10
  589.0 4.0 reduce-scatter.21.cloned.1.call-done
  593.3 66.7 %reduce-scatter.13.cloned.1.call-done = bf16[128,3200]{1,0:T(8,128)(2,1)} async-done(((bf16[1024,3200]{1,0:T(8,128)(2,1)}), bf16[128,3200]{1,0:T(8,128)(2,1)}) %reduce-scatter.13.cloned.1.call-update) | async-done | bytes 819216 | tf_op jit(solution)/shard_map/reduce_scatter | solution.py:286
  660.0 10.2 %add_convert_fusion.2 = bf16[512,1024]{1,0:T(8,128)(2,1)} fusion(f32[512,1024]{1,0:T(8,128)S(1)} %copy-done.9, bf16[512,4096]{1,0:T(8,128)(2,1)} %get-tuple-element.29, bf16[4096,1024]{1,0:T(8,128)(2,1)} %bitcast.79, f32[1024]{0:T(1024)S(1)} %get-tuple-element.114), kind=kOutput, calls=%fused_computation.51 | convolution fusion | flops 4296540160 | bytes 15732736 | tf_op jit(solution)/shard_map/dot_general | solution.py:383
  670.3 11.9 %reduce-scatter.27.cloned.1.call-done = bf16[32,1152]{1,0:T(8,128)(2,1)} async-done(((bf16[128,1152]{1,0:T(8,128)(2,1)}), bf16[32,1152]{1,0:T(8,128)(2,1)}) %reduce-scatter.27.cloned.1.call-update) | async-done | bytes 73744
  688.9 3.2 add_convert_fusion.1
  692.1 17.7 %reduce-scatter.19.cloned.1.call-done = bf16[32,4096]{1,0:T(8,128)(2,1)} async-done(((bf16[128,4096]{1,0:T(8,128)(2,1)}), bf16[32,4096]{1,0:T(8,128)(2,1)}) %reduce-scatter.19.cloned.1.call-update) | async-done | bytes 262160 | tf_op jit(solution)/shard_map/reduce_scatter | solution.py:287
  711.7 26.5 %reduce-scatter.23.cloned.1.call-done = bf16[128,1024]{1,0:T(8,128)(2,1)} async-done(((bf16[512,1024]{1,0:T(8,128)(2,1)}), bf16[128,1024]{1,0:T(8,128)(2,1)}) %reduce-scatter.23.cloned.1.call-update) | async-done | bytes 262160 | tf_op jit(solution)/shard_map/reduce_scatter | solution.py:287
  739.9 22.7 %reduce-scatter.15.cloned.1.call-done = bf16[32,3200]{1,0:T(8,128)(2,1)} async-done(((bf16[128,3200]{1,0:T(8,128)(2,1)}), bf16[32,3200]{1,0:T(8,128)(2,1)}) %reduce-scatter.15.cloned.1.call-update) | async-done | bytes 204816 | tf_op jit(solution)/shard_map/reduce_scatter | solution.py:287
  (135 shorter events, 50.6 us)
Async XLA Ops:
  7.2 14.8 %copy-start.2 = (bf16[512,1024]{1,0:T(8,128)(2,1)S(1)}, bf16[512,1024]{1,0:T(8,128)(2,1)}, u32[]{:S(2)}) copy-start(bf16[512,1024]{1,0:T(8,128)(2,1)} %param.16) | copy-start | bytes 3145732
  7.2 82.3 %all-gather.3.cloned.1.call-start = ((), (), s32[]{:S(2)}) async-start(), calls=%async_computation.12 | async-start | bytes 6758400 | tf_op jit(solution)/shard_map/all_gather | solution.py:332
  15.9 292.5 %all-gather.5.cloned.1.call-start = ((), (), s32[]{:S(2)}) async-start(), calls=%async_computation.13 | async-start | bytes 19464192 | tf_op jit(solution)/shard_map/all_gather | solution.py:351
  21.1 0.8 copy-start.14
  113.4 4.8 copy-start.20
  113.4 129.3 %all-to-all-start = ((bf16[4,512,768]{1,2,0:T(8,128)(2,1)}), bf16[4,512,768]{1,2,0:T(8,128)(2,1)}, u32[]{:S(2)}, u32[]{:S(2)}) async-start(bf16[4,512,768]{1,2,0:T(8,128)(2,1)} %bitcast.74), calls=%async_computation | async-start | bytes 6291456 | tf_op jit(solution)/shard_map/all_to_all | solution.py:273
  281.6 26.8 %all-to-all-start.1 = ((bf16[4,512,256]{1,2,0:T(8,128)(2,1)}), bf16[4,512,256]{1,2,0:T(8,128)(2,1)S(1)}, u32[]{:S(2)}, u32[]{:S(2)}) async-start(bf16[4,512,256]{1,2,0:T(8,128)(2,1)} %copy.138), calls=%async_computation.1 | async-start | bytes 2097152 | tf_op jit(solution)/shard_map/all_to_all | solution.py:280
  285.1 302.5 %reduce-scatter.25.cloned.1.call-start = ((), (), s32[]{:S(2)}) async-start(), calls=%async_computation.20 | async-start | bytes 2654208
  308.3 1.0 copy-start.18
  312.6 66.1 %copy-start.8 = (f32[512,1024]{1,0:T(8,128)}, f32[512,1024]{1,0:T(8,128)S(1)}, u32[]{:S(2)}) copy-start(f32[512,1024]{1,0:T(8,128)S(1)} %get-tuple-element.150) | copy-start | bytes 6291460
  346.6 12.5 %copy-start.7 = (bf16[32,4,32,1024]{3,2,1,0:T(8,128)(2,1)S(1)}, bf16[32,4,32,1024]{3,2,1,0:T(8,128)(2,1)}, u32[]{:S(2)}) copy-start(bf16[32,4,32,1024]{3,2,1,0:T(8,128)(2,1)} %copy.139) | copy-start | bytes 25165828
  346.6 12.5 %copy-start.11 = (bf16[512,1024]{1,0:T(8,128)(2,1)S(1)}, bf16[512,1024]{1,0:T(8,128)(2,1)}, u32[]{:S(2)}) copy-start(bf16[512,1024]{1,0:T(8,128)(2,1)} %param.17) | copy-start | bytes 3145732
  366.2 2.0 copy-start.10
  387.5 3.1 copy-start.12
  389.9 1.4 copy-start
  390.6 1.6 copy-start.19
  391.2 1.0 copy-start.15
  399.3 189.1 %reduce-scatter.17.cloned.1.call-start = ((), (), s32[]{:S(2)}) async-start(), calls=%async_computation.16 | async-start | bytes 9437184 | tf_op jit(solution)/shard_map/reduce_scatter | solution.py:286
  399.8 193.2 %reduce-scatter.21.cloned.1.call-start = ((), (), s32[]{:S(2)}) async-start(), calls=%async_computation.18 | async-start | bytes 9437184 | tf_op jit(solution)/shard_map/reduce_scatter | solution.py:286
  408.9 1.3 copy-start.16
  414.0 5.3 copy-start.17
  415.2 30.2 %all-to-all-start.2 = ((bf16[4,512,256]{2,1,0:T(8,128)(2,1)}), bf16[4,512,256]{2,1,0:T(8,128)(2,1)S(1)}, u32[]{:S(2)}, u32[]{:S(2)}) async-start(bf16[4,512,256]{2,1,0:T(8,128)(2,1)} %bitcast.70), calls=%async_computation.2 | async-start | bytes 2097152 | tf_op jit(solution)/shard_map/all_to_all | solution.py:273
  419.3 240.7 %reduce-scatter.13.cloned.1.call-start = ((), (), s32[]{:S(2)}) async-start(), calls=%async_computation.14 | async-start | bytes 7372800 | tf_op jit(solution)/shard_map/reduce_scatter | solution.py:286
  445.4 1.8 copy-start.5
  568.8 1.4 copy-start.3
  569.0 7.2 copy-start.13
  576.2 1.3 copy-start.6
  576.2 2.0 copy-start.4
  587.5 72.5 %copy-start.9 = (f32[512,1024]{1,0:T(8,128)S(1)}, f32[512,1024]{1,0:T(8,128)}, u32[]{:S(2)}) copy-start(f32[512,1024]{1,0:T(8,128)} %copy-done.8) | copy-start | bytes 6291460
  587.5 94.7 %reduce-scatter.27.cloned.1.call-start = ((), (), s32[]{:S(2)}) async-start(), calls=%async_computation.21 | async-start | bytes 368640
  588.2 121.6 %reduce-scatter.19.cloned.1.call-start = ((), (), s32[]{:S(2)}) async-start(), calls=%async_computation.17 | async-start | bytes 1310720 | tf_op jit(solution)/shard_map/reduce_scatter | solution.py:287
  589.0 149.1 %reduce-scatter.23.cloned.1.call-start = ((), (), s32[]{:S(2)}) async-start(), calls=%async_computation.19 | async-start | bytes 1310720 | tf_op jit(solution)/shard_map/reduce_scatter | solution.py:287
  593.0 169.5 %reduce-scatter.15.cloned.1.call-start = ((), (), s32[]{:S(2)}) async-start(), calls=%async_computation.15 | async-start | bytes 1024000 | tf_op jit(solution)/shard_map/reduce_scatter | solution.py:287
  670.3 18.6 %copy-start.1 = (f32[512,1024]{1,0:T(8,128)S(1)}, f32[512,1024]{1,0:T(8,128)}, u32[]{:S(2)}) copy-start(f32[512,1024]{1,0:T(8,128)} %copy-done) | copy-start | bytes 6291460
Sparse Core Ops, SparseCore 0:
  16.0 73.4 all-gather.2
  92.3 176.3 all-gather.4
  399.4 43.9 reduce-scatter.24
  447.1 71.2 reduce-scatter.16
  521.7 71.2 reduce-scatter.20
  596.7 63.2 reduce-scatter.12
  662.3 19.8 reduce-scatter.26
  684.4 25.3 reduce-scatter.18
  712.3 25.7 reduce-scatter.22
  740.3 22.2 reduce-scatter.14
